TPU v7x, 32 devices: a whole 2x2x4 slice. The times are simulated.
32 devices in a mesh: groups: 2 (over y), dev: 8 (over z, x), sub: 2 (over core).
Axes of the slice: x: 2, y: 2, z: 4, core: 2. Of those that a mesh axis runs over, the one named last changes fastest.
Arguments:
- tokens: bfloat16 [2048, 2048], P(('groups', 'dev')), parts along dimension 0, may hold values from -6 to 6
- query_key_value: bfloat16 [2048, 3, 2048], P(('groups', 'dev'), None, 'sub'), parts along dimension 0, may hold values from -6 to 6
- out_weight: bfloat16 [2048, 2048], P('dev', 'sub'), may hold values from -0.125 to 0.125
- modulation: float32 [8, 2048], P('groups'), parts along dimension 0, may hold values from -3 to 3
- router_weight: bfloat16 [2048, 64], replicated, may hold values from -0.125 to 0.125
- expert_ids: int32 [2048, 4], P(('groups', 'dev')), parts along dimension 0, may hold values from 0 to 63, all different within a row; in each aligned block of 128 rows (0 to 127, 128 to 255, ...) at most 12 rows name the same one
- gate_up_weight: bfloat16 [128, 2, 2048, 384], P('dev', None, None, 'sub'), may hold values from -0.125 to 0.125
- down_weight: bfloat16 [128, 384, 2048], P('dev', None, 'sub'), may hold values from -0.21875 to 0.21875
Outputs:
- block_out: bfloat16 [2048, 2048], P(('groups', 'dev'), 'sub'), parts along dimension 0
There are 2 independent parts, one for each index of `groups`. A program takes and returns all parts, laid end to end along the dimension named above; an argument that names none is the same for every part. Nothing has to cross between parts.
Inputs may be any that keep to these rules, and one draw needn't show every extreme that they name: `expert_ids`: each token names 4 different experts. Within each aligned block of 128 rows no expert is named by more than 12 rows, a bound that some block reaches.
All inputs are finite; a program needn't handle non-finite values.
Results may differ from a plain program's by a relative error of at most 0.008.
Values may be sent and summed in bfloat16 or wider, within the bound.
A program may use at most 128 MiB of HBM per device.

v0:
```python
import math

import jax
import jax.numpy as jnp
from jax import lax
from jax.sharding import PartitionSpec as P

HEAD = 128
CAP = 12


EPS = 1e-06
NEG = -1e30


def extended(cells, sides, width):
    for axis, dim in sides:
        count = lax.axis_size(axis)
        ends = count - 1
        head = lax.slice_in_dim(cells, 0, width, axis=dim)
        tail = lax.slice_in_dim(cells, cells.shape[dim] - width, cells.shape[dim], axis=dim)
        cells = jnp.concatenate(
            [
                lax.ppermute(tail, axis, [(i, (i + 1) % count) for i in range(ends)]),
                cells,
                lax.ppermute(head, axis, [((i + 1) % count, i) for i in range(ends)]),
            ],
            axis=dim,
        )
    return cells


def window_attention(query, keys, values, index, total):
    count = query.shape[0]
    rows = jnp.arange(count, dtype=jnp.int32)[:, None]
    cols = jnp.arange(3 * count, dtype=jnp.int32)[None, :] - count
    place = index * count + cols
    allowed = (jnp.abs(cols - rows) <= count) & (place >= 0) & (place < total)
    scores = jnp.einsum(
        "qhd,khd->hqk", query, keys, preferred_element_type=jnp.float32
    ) / math.sqrt(query.shape[2])
    scores = jnp.where(allowed[None], scores, NEG)
    top = jnp.max(scores, -1, keepdims=True)
    weight = jnp.exp(scores - top)
    weight = (weight / jnp.sum(weight, -1, keepdims=True)).astype(jnp.bfloat16)
    mixed = jnp.einsum("hqk,khd->qhd", weight, values, preferred_element_type=jnp.float32)
    return mixed.astype(jnp.bfloat16)


def normalize(state, modulation):
    scale = lax.rsqrt(jnp.mean(state * state, -1, keepdims=True) + EPS)
    return (state * scale * (1.0 + modulation[2]) + modulation[1]).astype(jnp.bfloat16)


def route(normed, router_weight, expert_ids):
    logits = jnp.dot(normed, router_weight, preferred_element_type=jnp.float32)
    experts = router_weight.shape[1]
    match = expert_ids[:, :, None] == jnp.arange(experts, dtype=jnp.int32)[None, None, :]
    picked = jnp.sum(jnp.where(match, logits[:, None, :], 0.0), -1)
    lifted = jax.nn.sigmoid(picked)
    return lifted / jnp.sum(lifted, -1, keepdims=True)


def body(
    tokens,
    query_key_value,
    out_weight,
    modulation,
    router_weight,
    expert_ids,
    gate_up_weight,
    down_weight,
):
    count = tokens.shape[0]
    width = tokens.shape[1]
    parts = lax.axis_size("sub")
    part = lax.axis_index("sub")
    position = lax.axis_index("dev")
    devices = lax.axis_size("dev")
    total = count * devices
    local_width = query_key_value.shape[2]
    heads_here = local_width // HEAD
    query = query_key_value[:, 0].reshape(count, heads_here, HEAD)
    pair = query_key_value[:, 1:]
    near = extended(pair, (("dev", 0),), count)
    keys = near[:, 0].reshape(3 * count, heads_here, HEAD)
    values = near[:, 1].reshape(3 * count, heads_here, HEAD)
    mixed = window_attention(query, keys, values, position, total).reshape(count, local_width)
    partial_proj = lax.dot_general(
        mixed,
        lax.all_gather(out_weight, "dev", axis=0, tiled=True),
        (((1,), (1,)), ((), ())),
        preferred_element_type=jnp.float32,
    )
    proj = lax.psum(partial_proj, "sub")
    state = tokens.astype(jnp.float32) + (1.0 + modulation[0]) * proj
    normed = normalize(state, modulation)
    gates = route(normed, router_weight, expert_ids)
    experts = router_weight.shape[1]
    topk = expert_ids.shape[1]
    flat = expert_ids.reshape(-1)
    picks = flat.shape[0]
    onehot = (flat[:, None] == jnp.arange(experts, dtype=jnp.int32)[None, :]).astype(jnp.int32)
    rank = jnp.sum((jnp.cumsum(onehot, 0) - 1) * onehot, 1)
    target = flat * CAP + rank
    hit = target[None, :] == jnp.arange(experts * CAP, dtype=jnp.int32)[:, None]
    filled = jnp.any(hit, 1)
    anchor = jnp.sum(jnp.where(hit, jnp.arange(picks, dtype=jnp.int32)[None, :], 0), 1) // topk
    slice_width = width // parts
    sent = lax.dynamic_slice_in_dim(normed, part * slice_width, slice_width, 1)
    sent_width = sent.shape[1]
    rows_out = jnp.where(filled[:, None], sent[anchor], jnp.zeros((), jnp.bfloat16))
    halves_here = gate_up_weight.shape[0]
    doubled = jnp.broadcast_to(
        rows_out.reshape(experts, 1, CAP, sent_width), (experts, 2, CAP, sent_width)
    )
    outgoing = doubled.reshape(devices, halves_here, CAP, sent_width)
    up_form = "sxcd,xgdf->sxcgf"
    down_form = "sxcf,xfd->sxcd"
    incoming = lax.all_to_all(outgoing, "dev", split_axis=0, concat_axis=0, tiled=True)
    both = jnp.einsum(
        up_form,
        lax.all_gather(incoming, "sub", axis=3, tiled=True),
        gate_up_weight,
        preferred_element_type=jnp.float32,
    )
    hidden = (jax.nn.silu(both[..., 0, :]) * both[..., 1, :]).astype(jnp.bfloat16)
    gathered = lax.all_gather(hidden, "sub", axis=hidden.ndim - 1, tiled=True)
    result = jnp.einsum(down_form, gathered, down_weight, preferred_element_type=jnp.float32)
    returned = lax.all_to_all(
        result.astype(jnp.bfloat16), "dev", split_axis=0, concat_axis=0, tiled=True
    )
    own_width = returned.shape[-1]
    arranged = returned.reshape(experts, 2, CAP, own_width)
    answers = arranged[flat, :, rank, :].reshape(count, topk, 2, own_width).astype(jnp.float32)
    combined = answers[:, :, 0] + answers[:, :, 1]
    routed = jnp.einsum("tk,tkd->td", gates, combined)
    own = lax.dynamic_slice_in_dim(state, part * slice_width, slice_width, 1)
    lift = lax.dynamic_slice_in_dim(modulation[3], part * slice_width, slice_width, 0)
    return (own + (1.0 + lift) * routed).astype(jnp.bfloat16)


def solution(mesh):
    return jax.shard_map(
        body,
        mesh=mesh,
        in_specs=(
            P(("groups", "dev"), None),
            P(("groups", "dev"), None, "sub"),
            P("dev", "sub"),
            P("groups", None),
            P(),
            P(("groups", "dev"), None),
            P("dev", None, None, "sub"),
            P("dev", None, "sub"),
        ),
        out_specs=P(("groups", "dev"), "sub"),
        check_vma=False,
    )
```

profile of v0, /device:TPU:0, one launch (start us, length us, event | category | flops | bytes accessed | tf_op | source)
XLA Modules:
  0.0 426.2 jit_solution(14000772186241778304)
XLA Ops:
  6.5 0.7 all-gather.4.cloned.1.call-update
  7.3 1.1 slice.43
  8.4 0.3 copy.77
  8.7 1.3 collective-permute-start.1
  10.0 5.5 %collective-permute-start = (bf16[128,2,1024]{0,2,1:T(8,128)(2,1)S(1)}, bf16[128,2,1024]{0,2,1:T(8,128)(2,1)S(1)}, u32[]{:S(2)}, u32[]{:S(2)}) collective-permute-start(bf16[128,2,1024]{0,2,1:T(8,128)(2,1)S(1)} %copy.77), channel_id=1, source_target_pairs={{0,2},{2,4},{4,6},{6,8},{8,10},{10,12},{12,14},{1,3},{3,5},{5,7},{... | collective-permute-start | bytes 1572872 | tf_op jit(solution)/shard_map/ppermute | solution.py:24
  15.9 1.2 reduce-window.6
  17.1 0.2 slice_reduce_fusion
  17.9 10.8 %collective-permute-done.1 = bf16[128,2,1024]{0,2,1:T(8,128)(2,1)S(1)} collective-permute-done((bf16[128,2,1024]{0,2,1:T(8,128)(2,1)S(1)}, bf16[128,2,1024]{0,2,1:T(8,128)(2,1)S(1)}, u32[]{:S(2)}, u32[]{:S(2)}) %collective-permute-start.1) | collective-permute-done | bytes 524320 | tf_op jit(solution)/shard_map/ppermute | solution.py:26
  28.7 13.7 %collective-permute-done = bf16[128,2,1024]{0,2,1:T(8,128)(2,1)S(1)} collective-permute-done((bf16[128,2,1024]{0,2,1:T(8,128)(2,1)S(1)}, bf16[128,2,1024]{0,2,1:T(8,128)(2,1)S(1)}, u32[]{:S(2)}, u32[]{:S(2)}) %collective-permute-start) | collective-permute-done | bytes 524320 | tf_op jit(solution)/shard_map/ppermute | solution.py:24
  42.8 1.9 fusion.39
  44.7 1.8 convolution_convert_fusion
  46.5 48.6 %all-gather.4.cloned.1.call-done = bf16[2048,1024]{1,0:T(8,128)(2,1)} async-done(((bf16[256,1024]{1,0:T(8,128)(2,1)}), bf16[2048,1024]{1,0:T(8,128)(2,1)}) %all-gather.4.cloned.1.call-update) | async-done | bytes 4194320 | tf_op jit(solution)/shard_map/all_gather | solution.py:91
  95.0 4.7 %fusion.40 = f32[128,2048]{1,0:T(8,128)} fusion(bf16[128,1024]{0,1:T(8,128)(2,1)S(1)} %bitcast.105, bf16[2048,1024]{1,0:T(8,128)(2,1)} %all-gather.4.cloned.1.call-done), kind=kOutput, calls=%fused_computation.79 | convolution fusion | flops 536870912 | bytes 5505024 | tf_op jit(solution)/shard_map/dot_general | solution.py:89
  99.9 0.2 fusion.19
  100.2 0.2 select_reduce_fusion
  100.6 17.4 %all-reduce.2.cloned.1.call-done = f32[128,2048]{1,0:T(8,128)} async-done(((f32[128,2048]{1,0:T(8,128)}), f32[128,2048]{1,0:T(8,128)}) %all-reduce.2.cloned.1.call-update) | async-done | bytes 1048592 | tf_op jit(solution)/shard_map/psum | solution.py:95
  117.9 1.5 multiply_reduce_fusion
  119.4 1.0 copy-done.1
  120.6 0.8 copy-done.3
  121.4 3.6 gather_fusion
  125.0 2.4 gather.9
  127.4 0.2 broadcast_select_fusion
  127.6 2.0 copy.58
  129.6 3.7 broadcast_in_dim.85
  133.3 3.3 reshape.240
  136.6 2.4 copy.59
  139.0 76.7 %all_to_all.10 = bf16[8,16,12,1024]{3,1,2,0:T(8,128)(2,1)S(1)} all-to-all(bf16[8,16,12,1024]{3,1,2,0:T(8,128)(2,1)S(1)} %copy.59), channel_id=1, replica_groups=mesh['groups'=2,'dev'=8,'sub'=2] {'dev'}, dimensions={0} | all-to-all | bytes 6291456 | tf_op jit(solution)/shard_map/all_to_all | solution.py:120
  215.7 3.8 copy.60
  219.8 18.8 %all-gather.6.cloned.1.call-done = bf16[8,16,12,2048]{3,2,0,1:T(8,128)(2,1)} async-done(((bf16[8,16,12,1024]{3,2,0,1:T(8,128)(2,1)}), bf16[8,16,12,2048]{3,2,0,1:T(8,128)(2,1)}) %all-gather.6.cloned.1.call-update) | async-done | bytes 6291472 | tf_op jit(solution)/shard_map/all_gather | solution.py:123
  238.6 15.0 %fusion.8 = f32[8,16,12,2,192]{4,2,3,0,1:T(8,128)S(1)} fusion(bf16[16,2,2048,192]{2,3,1,0:T(8,128)(2,1)} %param.14, bf16[8,16,12,2048]{3,2,0,1:T(8,128)(2,1)} %all-gather.6.cloned.1.call-done), kind=kOutput, calls=%fused_computation.9 | convolution fusion | flops 2415919104 | bytes 33816576 | tf_op jit(solution)/shard_map/sxcd,xgdf->sxcgf/dot_general | solution.py:121
  253.6 0.7 fusion.14
  254.3 11.8 %copy.62 = bf16[8,16,12,192]{1,0,2,3:T(8,128)(2,1)} copy(bf16[8,16,12,192]{3,2,0,1:T(8,128)(2,1)S(1)} %fusion.14) | data formatting | bytes 1179648 | tf_op jit(solution)/shard_map/convert_element_type | solution.py:127
  266.2 22.9 %all-gather.8.cloned.1.call-done = bf16[8,16,12,384]{1,0,2,3:T(8,128)(2,1)} async-done(((bf16[8,16,12,192]{1,0,2,3:T(8,128)(2,1)}), bf16[8,16,12,384]{1,0,2,3:T(8,128)(2,1)}) %all-gather.8.cloned.1.call-update) | async-done | bytes 1179664 | tf_op jit(solution)/shard_map/all_gather | solution.py:128
  289.1 17.8 %copy.63 = bf16[8,16,12,384]{3,2,0,1:T(8,128)(2,1)S(1)} copy(bf16[8,16,12,384]{1,0,2,3:T(8,128)(2,1)} %all-gather.8.cloned.1.call-done) | data formatting | bytes 2359296 | tf_op jit(solution)/shard_map/all_gather | solution.py:128
  306.9 6.9 %convert_bitcast_fusion = bf16[8,16,12,1024]{3,2,0,1:T(8,128)(2,1)S(1)} fusion(bf16[8,16,12,384]{3,2,0,1:T(8,128)(2,1)S(1)} %copy.63, bf16[16,384,1024]{2,1,0:T(8,128)(2,1)} %param.15), kind=kOutput, calls=%fused_computation.8 | convolution fusion | flops 1209532416 | bytes 16908288 | tf_op jit(solution)/shard_map/sxcf,xfd->sxcd/dot_general | solution.py:129
  313.8 3.5 copy.64
  317.3 5.8 %all-to-all-start.1 = ((bf16[8,16,12,1024]{3,1,2,0:T(8,128)(2,1)}), bf16[8,16,12,1024]{3,1,2,0:T(8,128)(2,1)S(1)}, u32[]{:S(2)}, u32[]{:S(2)}) async-start(bf16[8,16,12,1024]{3,1,2,0:T(8,128)(2,1)} %copy.64), calls=%async_computation.1 | async-start | bytes 6291456 | tf_op jit(solution)/shard_map/all_to_all | solution.py:130
  323.2 1.3 fusion.41
  324.8 69.4 %all-to-all-done.1 = bf16[8,16,12,1024]{3,1,2,0:T(8,128)(2,1)S(1)} async-done(((bf16[8,16,12,1024]{3,1,2,0:T(8,128)(2,1)}), bf16[8,16,12,1024]{3,1,2,0:T(8,128)(2,1)S(1)}, u32[]{:S(2)}, u32[]{:S(2)}) %all-to-all-start.1) | async-done | bytes 3145760 | tf_op jit(solution)/shard_map/all_to_all | solution.py:130
  394.2 2.0 copy.65
  396.2 4.0 reshape.241
  400.3 5.2 %copy.67 = bf16[64,2,12,1024]{3,1,2,0:T(2,128)(2,1)} copy(bf16[64,2,12,1024]{3,1,0,2:T(2,128)(2,1)S(1)} %reshape.241) | data formatting | bytes 6291456 | tf_op jit(solution)/shard_map/reshape | solution.py:134
  405.4 7.5 %gather_fusion.1 = bf16[512,2,1024]{2,1,0:T(2,128)(2,1)S(1)} fusion(bf16[64,2,12,1024]{3,1,2,0:T(2,128)(2,1)} %copy.67, s32[512]{0:T(512)S(1)} %bitcast.100), kind=kCustom, calls=%fused_computation.1 | custom fusion | bytes 4198400 | tf_op jit(solution)/shard_map/gather | solution.py:135
  413.0 2.0 convert.1
  415.0 2.7 slice_add_fusion
  417.6 0.7 fusion.15
  418.3 0.5 copy-done.2
  418.8 0.8 fusion.22
  (48 shorter events, 2.4 us)
Async XLA Ops:
  6.5 316.7 %copy-start = (bf16[2048,64]{0,1:T(8,128)(2,1)S(1)}, bf16[2048,64]{0,1:T(8,128)(2,1)}, u32[]{:S(2)}) copy-start(bf16[2048,64]{0,1:T(8,128)(2,1)} %param.12) | copy-start | bytes 786436
  6.5 10.8 %slice-start = ((bf16[128,3,1024]{2,0,1:T(8,128)(2,1)}), bf16[128,1,1024]{2,0,1:T(8,128)(2,1)S(1)}, s32[]{:S(2)}) async-start(bf16[128,3,1024]{2,0,1:T(8,128)(2,1)} %param.9), calls=%async_computation.6 | async-start | bytes 524288 | tf_op jit(solution)/shard_map/slice | solution.py:83
  6.5 9.0 %copy-start.6 = (s32[128,4]{0,1:T(4,128)S(1)}, s32[128,4]{0,1:T(4,128)}, u32[]{:S(2)}) copy-start(s32[128,4]{0,1:T(4,128)} %param.13) | copy-start | bytes 6148
  6.5 88.5 %all-gather.4.cloned.1.call-start = ((), (), s32[]{:S(2)}) async-start(), calls=%async_computation.2 | async-start | bytes 4718592 | tf_op jit(solution)/shard_map/all_gather | solution.py:91
  7.3 110.7 %all-reduce.2.cloned.1.call-start = ((), (), s32[]{:S(2)}) async-start(), calls=%async_computation.3 | async-start | bytes 2097152 | tf_op jit(solution)/shard_map/psum | solution.py:95
  8.7 20.1 %collective-permute-start.1 = (bf16[128,2,1024]{0,2,1:T(8,128)(2,1)S(1)}, bf16[128,2,1024]{0,2,1:T(8,128)(2,1)S(1)}, u32[]{:S(2)}, u32[]{:S(2)}) collective-permute-start(bf16[128,2,1024]{0,2,1:T(8,128)(2,1)S(1)} %copy.77), channel_id=1, source_target_pairs={{2,0},{4,2},{6,4},{8,6},{10,8},{12,10},{14,12},{3,1},{5,3},{7,5},{... | collective-permute-start | bytes 1572872 | tf_op jit(solution)/shard_map/ppermute | solution.py:26
  10.0 32.5 %collective-permute-start = (bf16[128,2,1024]{0,2,1:T(8,128)(2,1)S(1)}, bf16[128,2,1024]{0,2,1:T(8,128)(2,1)S(1)}, u32[]{:S(2)}, u32[]{:S(2)}) collective-permute-start(bf16[128,2,1024]{0,2,1:T(8,128)(2,1)S(1)} %copy.77), channel_id=1, source_target_pairs={{0,2},{2,4},{4,6},{6,8},{8,10},{10,12},{12,14},{1,3},{3,5},{5,7},{... | collective-permute-start | bytes 1572872 | tf_op jit(solution)/shard_map/ppermute | solution.py:24
  95.0 5.5 %copy-start.5 = (f32[4,2048]{1,0:T(4,128)S(1)}, f32[4,2048]{1,0:T(4,128)}, u32[]{:S(2)}) copy-start(f32[4,2048]{1,0:T(4,128)} %param.11) | copy-start | bytes 98308
  95.0 22.9 %copy-start.4 = (bf16[128,2048]{1,0:T(8,128)(2,1)S(1)}, bf16[128,2048]{1,0:T(8,128)(2,1)}, u32[]{:S(2)}) copy-start(bf16[128,2048]{1,0:T(8,128)(2,1)} %param.8) | copy-start | bytes 1572868
  99.8 138.8 %all-gather.6.cloned.1.call-start = ((), (), s32[]{:S(2)}) async-start(), calls=%async_computation.4 | async-start | bytes 12582912 | tf_op jit(solution)/shard_map/all_gather | solution.py:123
  119.4 1.0 copy-start.1
  120.6 0.8 copy-start.3
  219.5 69.5 %all-gather.8.cloned.1.call-start = ((), (), s32[]{:S(2)}) async-start(), calls=%async_computation.5 | async-start | bytes 14155776 | tf_op jit(solution)/shard_map/all_gather | solution.py:128
  317.3 76.9 %all-to-all-start.1 = ((bf16[8,16,12,1024]{3,1,2,0:T(8,128)(2,1)}), bf16[8,16,12,1024]{3,1,2,0:T(8,128)(2,1)S(1)}, u32[]{:S(2)}, u32[]{:S(2)}) async-start(bf16[8,16,12,1024]{3,1,2,0:T(8,128)(2,1)} %copy.64), calls=%async_computation.1 | async-start | bytes 6291456 | tf_op jit(solution)/shard_map/all_to_all | solution.py:130
  417.6 1.2 copy-start.2
Sparse Core Ops, SparseCore 0:
  9.5 85.5 all-gather.3
  99.9 17.9 all-reduce.1
  219.7 18.8 all-gather.5
  266.3 22.7 all-gather.7
where the time goes:
time: 427 us; the launch traced here: 426 us
  waiting for transfers between devices  202 us (47%)
  local copies, waits for them, and re-layouts  77.9 us (18%)
  blocking collectives  76.7 us (18%)
  matrix products  32.4 us (8%)
  between operations  13.5 us (3%)
  starting transfers between devices  12.9 us (3%)
  other arithmetic  10.5 us (2%)
    all_to_all x1, blocking collectives, body(): lax.all_to_all(outgoing, 'dev', split_axis=0, concat_axis=0, tiled=True)  76.7 us
    all_to_all x1, waiting for transfers between devices, body(): lax.all_to_all(result.astype(jnp.bfloat16), 'dev', split_axis=0, concat_a...  69.4 us
    all_gather x1, waiting for transfers between devices, body(): lax.all_gather(out_weight, 'dev', axis=0, tiled=True)  48.6 us
    all_gather x1, waiting for transfers between devices, body(): gathered = lax.all_gather(hidden, 'sub', axis=hidden.ndim - 1, tiled=True)  22.9 us
    all_gather x1, waiting for transfers between devices, body(): lax.all_gather(incoming, 'sub', axis=3, tiled=True)  18.8 us
    all_gather x1, local copies, waits for them, and re-layouts, body(): gathered = lax.all_gather(hidden, 'sub', axis=hidden.ndim - 1, tiled=True)  17.8 us
    psum x1, waiting for transfers between devices, body(): proj = lax.psum(partial_proj, 'sub')  17.4 us
    dot_general x1, matrix products, body(): jnp.einsum(up_form, lax.all_gather(incoming, 'sub', axis=3, tiled=True),...  15 us
  transfers between devices with their start and end apart: 7, of which 7 were waited for; matrix products, arithmetic and copies ran while one was open for 2% of the time, Pallas kernels for 0%

commit v1 on v0

--- a/solution.py
+++ b/solution.py
@@ -1,8 +1,11 @@
+import functools
 import math
 
 import jax
 import jax.numpy as jnp
 from jax import lax
+from jax.experimental import pallas as pl
+from jax.experimental.pallas import tpu as pltpu
 from jax.sharding import PartitionSpec as P
 
 HEAD = 128
@@ -59,6 +62,371 @@
     picked = jnp.sum(jnp.where(match, logits[:, None, :], 0.0), -1)
     lifted = jax.nn.sigmoid(picked)
     return lifted / jnp.sum(lifted, -1, keepdims=True)
+
+
+LANES = 128
+SLOT = 16
+COLS = 2
+VMEM_BYTES = 66 * 1000 * 1000
+MESH = pl.DeviceIdType.MESH
+
+
+def expert_kernel(
+    rows_of, devices,
+    normed, meta, state, modulation, gate_up, down,
+    out,
+    tok, disp, gu, dn, hid_own, hid_other, got_meta, pick, slot_gate, got_x, got_up, got_down, acc,
+    meta_s, meta_r, ag_s, ag_r, core_r, gu_sem, dn_sem, hid_s, hid_r,
+    x_s, x_r, up_s, up_r, down_s, down_r,
+):
+    me = lax.axis_index("dev")
+    part = lax.axis_index("sub")
+    other = 1 - part
+    z = me // COLS
+    x = me % COLS
+    across = z * COLS + (1 - x)
+    lines = devices // COLS
+    count, width = normed.shape
+    half = width // 2
+    halves = gate_up.shape[0]
+    local = halves // 2
+    hidden = gate_up.shape[2]
+    slots = local * SLOT
+
+    def weight_copies(h):
+        return (
+            pltpu.make_async_copy(gate_up.at[h], gu.at[h], gu_sem.at[h]),
+            pltpu.make_async_copy(down.at[h], dn.at[h], dn_sem.at[h]),
+        )
+
+    barrier = pltpu.get_barrier_semaphore()
+    for step in range(1, devices):
+        pl.semaphore_signal(
+            barrier, inc=1, device_id={"dev": (me + step) % devices}, device_id_type=MESH
+        )
+    pl.semaphore_signal(barrier, inc=1, device_id={"sub": other}, device_id_type=MESH)
+    pl.semaphore_wait(barrier, devices)
+
+    def remote(src, dst, send, recv, where):
+        return pltpu.make_async_remote_copy(
+            src_ref=src, dst_ref=dst, send_sem=send, recv_sem=recv,
+            device_id=where, device_id_type=MESH,
+        )
+
+    def block(s, way, where, src=None):
+        dst = tok.at[part, s]
+        recv = core_r.at[s] if way == 3 else ag_r.at[s]
+        return remote(dst if src is None else src, dst, ag_s.at[s, way], recv, where)
+
+    up_to = {"dev": jnp.minimum(me + COLS, devices - 1)}
+    down_to = {"dev": jnp.maximum(me - COLS, 0)}
+    x_to = {"dev": across}
+    core_to = {"sub": other}
+    not_top = z < lines - 1
+    not_bottom = z > 0
+    mine = normed.at[:, pl.ds(pl.multiple_of(part * half, LANES), half)]
+
+    def meta_copy(step):
+        target = (me + step) % devices
+        return remote(
+            meta.at[pl.ds(pl.multiple_of(target * local, local), local)], got_meta.at[me],
+            meta_s.at[step - 1], meta_r.at[me], {"dev": target},
+        )
+
+    for step in range(1, devices):
+        meta_copy(step).start()
+
+    @pl.when(not_top)
+    def _():
+        block(me, 0, up_to, mine).start()
+
+    @pl.when(not_bottom)
+    def _():
+        block(me, 1, down_to, mine).start()
+
+    block(me, 2, x_to, mine).start()
+
+    def start_weights(h, carry):
+        for copy in weight_copies(h):
+            copy.start()
+        return carry
+
+    lax.fori_loop(0, halves, start_weights, 0)
+
+    before = (
+        lax.broadcasted_iota(jnp.int32, (count, count), 0)
+        < lax.broadcasted_iota(jnp.int32, (count, count), 1)
+    ).astype(jnp.float32).astype(jnp.bfloat16)
+    place = lax.broadcasted_iota(jnp.int32, (local, SLOT, count), 1).astype(jnp.float32)
+
+    def routing(s, gate):
+        chosen = jnp.where(gate > 0.0, 1.0, 0.0)
+        rank = jnp.dot(chosen.astype(jnp.bfloat16), before, preferred_element_type=jnp.float32)
+        rank = jnp.where(gate > 0.0, rank, -1.0)
+        hit = jnp.broadcast_to(rank[:, None, :], place.shape) == place
+        pick[s] = jnp.where(hit, 1.0, 0.0).reshape(slots, count).astype(jnp.bfloat16)
+        value = jnp.where(hit, jnp.broadcast_to(gate[:, None, :], place.shape), 0.0)
+        value = jnp.sum(value, -1, keepdims=True)
+        slot_gate[:, pl.ds(pl.multiple_of(s * SLOT, SLOT), SLOT), :] = jnp.broadcast_to(
+            value, (local, SLOT, LANES)
+        )
+
+    def dispatch(s, h, rows):
+        moved = jnp.dot(pick[s], rows, preferred_element_type=jnp.float32)
+        disp[h, :, pl.ds(pl.multiple_of(s * SLOT, SLOT), SLOT), :] = moved.astype(
+            jnp.bfloat16
+        ).reshape(local, SLOT, half)
+
+    routing(me, meta[pl.ds(pl.multiple_of(me * local, local), local)])
+    dispatch(me, 0, normed[:, :half])
+    dispatch(me, 1, normed[:, half:])
+    for step in range(1, devices):
+        s = (me + step) % devices
+        remote(
+            meta.at[pl.ds(0, local)], got_meta.at[s], meta_s.at[0], meta_r.at[s], {"dev": s}
+        ).wait_recv()
+        routing(s, got_meta[s])
+
+    def arrive(s):
+        block(s, 2, x_to).wait_recv()
+
+    def from_line(zz, way, where, more):
+        s = zz * COLS + x
+        arrive(s)
+
+        @pl.when(more)
+        def _():
+            block(s, way, where).start()
+
+        block(s, 2, x_to).start()
+        block(s, 3, core_to).start()
+        dispatch(s, part, tok[part, s])
+
+    def from_across(zz):
+        s = zz * COLS + (1 - x)
+        arrive(s)
+        block(s, 3, core_to).start()
+        dispatch(s, part, tok[part, s])
+
+    def from_core(s):
+        remote(tok.at[other, s], tok.at[other, s], ag_s.at[s, 3], core_r.at[s], core_to).wait_recv()
+        dispatch(s, other, tok[other, s])
+
+    def both(d, act):
+        @pl.when(z - d >= 0)
+        def _():
+            act(z - d, True)
+
+        @pl.when(z + d < lines)
+        def _():
+            act(z + d, False)
+
+    for d in range(1, lines):
+        both(d, lambda zz, low: from_line(
+            zz, 0 if low else 1, up_to if low else down_to, not_top if low else not_bottom
+        ))
+        if d == 1:
+            from_across(z)
+        else:
+            both(d - 1, lambda zz, low: from_core(zz * COLS + x))
+    both(lines - 1, lambda zz, low: from_core(zz * COLS + x))
+    from_core(across)
+    for d in range(1, lines):
+        both(d, lambda zz, low: from_across(zz))
+        if d > 1:
+            both(d - 1, lambda zz, low: from_core(zz * COLS + (1 - x)))
+    both(lines - 1, lambda zz, low: from_core(zz * COLS + (1 - x)))
+
+    @pl.when(not_top)
+    def _():
+        block(me, 0, up_to, mine).wait_send()
+
+    @pl.when(not_bottom)
+    def _():
+        block(me, 1, down_to, mine).wait_send()
+
+    block(me, 2, x_to, mine).wait_send()
+    for d in range(1, lines):
+
+        def sent(zz, low):
+            s = zz * COLS + x
+
+            @pl.when(not_top if low else not_bottom)
+            def _():
+                block(s, 0 if low else 1, up_to).wait_send()
+
+            block(s, 2, x_to).wait_send()
+            block(s, 3, core_to).wait_send()
+            block(zz * COLS + (1 - x), 3, core_to).wait_send()
+
+        both(d, sent)
+    block(across, 3, core_to).wait_send()
+
+    def hid_copy(h):
+        return remote(hid_own.at[h], hid_other.at[h], hid_s.at[h], hid_r.at[h], core_to)
+
+    def across_rows(left, right):
+        return lax.dot_general(
+            left, right, (((1,), (1,)), ((), ())), preferred_element_type=jnp.float32
+        )
+
+    def raise_expert(e):
+        low, high = disp[0, e], disp[1, e]
+        for b in range(2):
+            h = 2 * e + b
+            weight_copies(h)[0].wait()
+
+            def product(g):
+                return across_rows(low, gu[h, g, :, :half]) + across_rows(high, gu[h, g, :, half:])
+
+            gate = product(0)
+            hid_own[h] = (gate * jax.nn.sigmoid(gate) * product(1)).astype(jnp.bfloat16)
+            hid_copy(h).start()
+
+    def lower_expert(e):
+        total = None
+        for b in range(2):
+            h = 2 * e + b
+            weight_copies(h)[1].wait()
+            hid_copy(h).wait_recv()
+            first = dn[h, pl.ds(pl.multiple_of(part * hidden, SLOT), hidden), :]
+            second = dn[h, pl.ds(pl.multiple_of(other * hidden, SLOT), hidden), :]
+            piece = jnp.dot(hid_own[h], first, preferred_element_type=jnp.float32) + jnp.dot(
+                hid_other[h], second, preferred_element_type=jnp.float32
+            )
+            piece = piece.astype(jnp.bfloat16).astype(jnp.float32)
+            total = piece if total is None else total + piece
+        gain = slot_gate[e][:, :1]
+        disp[0, e] = (total * gain).astype(jnp.bfloat16)
+
+    raise_expert(0)
+
+    def step_expert(e, carry):
+        raise_expert(e)
+        lower_expert(e - 1)
+        return carry
+
+    lax.fori_loop(1, local, step_expert, 0)
+    lower_expert(local - 1)
+
+    def combine(s):
+        rows = disp[0, :, pl.ds(pl.multiple_of(s * SLOT, SLOT), SLOT), :].reshape(slots, half)
+        return lax.dot_general(
+            pick[s], rows, (((0,), (0,)), ((), ())), preferred_element_type=jnp.float32
+        )
+
+    def x_copy(zz):
+        return remote(
+            tok.at[0, zz * COLS + (1 - x)], got_x.at[zz], x_s.at[zz], x_r.at[zz], x_to
+        )
+
+    def line_copy(zz, low):
+        if low:
+            return remote(tok.at[1, zz], got_down.at[zz], down_s.at[zz], down_r.at[zz], down_to)
+        return remote(tok.at[1, zz], got_up.at[zz], up_s.at[zz], up_r.at[zz], up_to)
+
+    def give_across(zz, low):
+        s = zz * COLS + (1 - x)
+        tok[0, s] = combine(s).astype(jnp.bfloat16)
+        x_copy(zz).start()
+
+    def add_line(zz, low):
+        line_copy(zz, low).wait_recv()
+        acc[...] += (got_down if low else got_up)[zz].astype(jnp.float32)
+
+    def gather_here(zz):
+        acc[...] = combine(zz * COLS + x)
+        x_copy(zz).wait_recv()
+        acc[...] += got_x[zz].astype(jnp.float32)
+
+    def pass_on(zz, low):
+        gather_here(zz)
+
+        @pl.when(not_top if low else not_bottom)
+        def _():
+            add_line(zz, low)
+
+        tok[1, zz] = acc[...].astype(jnp.bfloat16)
+        line_copy(zz, low).start()
+
+    for d in range(lines - 1, 0, -1):
+        both(d, give_across)
+    give_across(z, False)
+    for d in range(lines - 1, 0, -1):
+        both(d, pass_on)
+    gather_here(z)
+
+    @pl.when(not_bottom)
+    def _():
+        add_line(z, False)
+
+    @pl.when(not_top)
+    def _():
+        add_line(z, True)
+
+    own = pl.ds(pl.multiple_of(part * half, LANES), half)
+    out[...] = (state[:, own] + (1.0 + modulation[3:4, own]) * acc[...]).astype(out.dtype)
+
+    for d in range(1, lines):
+
+        def drained(zz, low):
+            line_copy(zz, low).wait_send()
+            x_copy(zz).wait_send()
+
+        both(d, drained)
+    x_copy(z).wait_send()
+    for step in range(1, devices):
+        meta_copy(step).wait_send()
+
+    def hid_drain(h, carry):
+        hid_copy(h).wait_send()
+        return carry
+
+    lax.fori_loop(0, halves, hid_drain, 0)
+
+
+def expert_call(normed, gates, expert_ids, state, modulation, gate_up_weight, down_weight, experts):
+    devices = lax.axis_size("dev")
+    count, width = normed.shape
+    half = down_weight.shape[2]
+    halves = gate_up_weight.shape[0]
+    local = halves // 2
+    gate_up_weight = gate_up_weight.swapaxes(2, 3)
+    hidden = gate_up_weight.shape[2]
+    lines = devices // COLS
+    rows = devices * SLOT
+    match = expert_ids[:, None, :] == jnp.arange(experts, dtype=jnp.int32)[None, :, None]
+    meta = jnp.sum(jnp.where(match, gates[:, None, :], 0.0), -1).T
+    vmem = pl.BlockSpec(memory_space=pltpu.VMEM)
+    hbm = pl.BlockSpec(memory_space=pl.ANY)
+    dma = pltpu.SemaphoreType.DMA
+    return pl.pallas_call(
+        functools.partial(expert_kernel, rows, devices),
+        out_shape=jax.ShapeDtypeStruct((count, half), jnp.bfloat16),
+        in_specs=[vmem, vmem, vmem, vmem, hbm, hbm],
+        out_specs=vmem,
+        scratch_shapes=[
+            pltpu.VMEM((2, devices, count, half), jnp.bfloat16),
+            pltpu.VMEM((2, local, rows, half), jnp.bfloat16),
+            pltpu.VMEM(gate_up_weight.shape, jnp.bfloat16),
+            pltpu.VMEM(down_weight.shape, jnp.bfloat16),
+            pltpu.VMEM((halves, rows, hidden), jnp.bfloat16),
+            pltpu.VMEM((halves, rows, hidden), jnp.bfloat16),
+            pltpu.VMEM((devices, local, count), jnp.float32),
+            pltpu.VMEM((devices, local * SLOT, count), jnp.bfloat16),
+            pltpu.VMEM((local, rows, LANES), jnp.float32),
+            pltpu.VMEM((lines, count, half), jnp.bfloat16),
+            pltpu.VMEM((lines, count, half), jnp.bfloat16),
+            pltpu.VMEM((lines, count, half), jnp.bfloat16),
+            pltpu.VMEM((count, half), jnp.float32),
+            dma((devices,)), dma((devices,)), dma((devices, 4)), dma((devices,)), dma((devices,)),
+            dma((halves,)), dma((halves,)), dma((halves,)), dma((halves,)),
+            dma((lines,)), dma((lines,)), dma((lines,)), dma((lines,)), dma((lines,)), dma((lines,)),
+        ],
+        compiler_params=pltpu.CompilerParams(
+            collective_id=1, has_side_effects=True, vmem_limit_bytes=VMEM_BYTES
+        ),
+    )(normed, meta, state, modulation, gate_up_weight, down_weight)
 
 
 def body(
@@ -97,6 +465,12 @@
     normed = normalize(state, modulation)
     gates = route(normed, router_weight, expert_ids)
     experts = router_weight.shape[1]
+    weight_bytes = 2 * (gate_up_weight.size + down_weight.size)
+    token_bytes = 10 * devices * count * width
+    if devices % COLS == 0 and parts == 2 and weight_bytes + token_bytes < VMEM_BYTES:
+        return expert_call(
+            normed, gates, expert_ids, state, modulation, gate_up_weight, down_weight, experts
+        )
     topk = expert_ids.shape[1]
     flat = expert_ids.reshape(-1)
     picks = flat.shape[0]

time: 427 us -> 210 us (0.49)
  waiting for transfers between devices: 202 us -> 95.5 us
  Pallas kernels: 0 us -> 79.5 us
  blocking collectives: 76.7 us -> 0 us
  local copies, waits for them, and re-layouts: 77.9 us -> 3.59 us
  matrix products: 32.4 us -> 8.72 us
  other arithmetic: 10.5 us -> 2.85 us
  starting transfers between devices: 12.9 us -> 6.24 us
    pallas_call x0 -> x1, Pallas kernels: none -> 79.5 us  [expert_call(): pl.pallas_call(functools.partial(expert_kernel, rows, devices), out_shape...]
    all_to_all x1 -> x0, blocking collectives: 76.7 us -> none  [body(): lax.all_to_all(outgoing, 'dev', split_axis=0, concat_axis=0, tiled=True)]
    all_to_all x1 -> x0, waiting for transfers between devices: 69.4 us -> none  [body(): lax.all_to_all(result.astype(jnp.bfloat16), 'dev', split_axis=0, concat_a...]
    all_gather x2 -> x0, waiting for transfers between devices: 41.7 us -> none  [the longest x1 22.9 us: body(): gathered = lax.all_gather(hidden, 'sub', axis=hidden.ndim - 1, tiled=True)]
    dot_general x3 -> x0, matrix products: 22.7 us -> none  [the longest x1 15 us: body(): jnp.einsum(up_form, lax.all_gather(incoming, 'sub', axis=3, tiled=True),...]
    all_gather x1 -> x0, local copies, waits for them, and re-layouts: 17.8 us -> none  [body(): gathered = lax.all_gather(hidden, 'sub', axis=hidden.ndim - 1, tiled=True)]
    convert_element_type x2 -> x0, local copies, waits for them, and re-layouts: 15.3 us -> none  [the longest x1 11.8 us: body(): (jax.nn.silu(both[..., 0, :]) * both[..., 1, :]).astype(jnp.bfloat16)]
    reshape x6 -> x0, local copies, waits for them, and re-layouts: 15.1 us -> none  [the longest x2 9.2 us: body(): arranged = returned.reshape(experts, 2, CAP, own_width)]
  transfers between devices with their start and end apart: 7 -> 4, of which waited for: 7 -> 3; matrix products, arithmetic and copies ran while one was open for 2% -> 2% of each run, Pallas kernels for 0% -> 0%
where the time goes in v1:
time: 210 us
  waiting for transfers between devices  95.5 us (45%)
  Pallas kernels  79.5 us (38%)
  between operations  13.6 us (6%)
  matrix products  8.72 us (4%)
  starting transfers between devices  6.24 us (3%)
  local copies, waits for them, and re-layouts  3.59 us (2%)
  other arithmetic  2.85 us (1%)
    pallas_call x1, Pallas kernels, expert_call(): pl.pallas_call(functools.partial(expert_kernel, rows, devices), out_shape...  79.5 us
    all_gather x1, waiting for transfers between devices, body(): lax.all_gather(out_weight, 'dev', axis=0, tiled=True)  50.4 us
    ppermute x1, waiting for transfers between devices, extended(): lax.ppermute(tail, axis, [(i, (i + 1) % count) for i in range(ends)])  26.2 us
    psum x1, waiting for transfers between devices, body(): proj = lax.psum(partial_proj, 'sub')  18.1 us
    ppermute x1, starting transfers between devices, extended(): lax.ppermute(tail, axis, [(i, (i + 1) % count) for i in range(ends)])  4.9 us
    dot_general x1, matrix products, body(): lax.dot_general(mixed, lax.all_gather(out_weight, 'dev', axis=0, tiled=Tr...  4.75 us
  transfers between devices with their start and end apart: 4, of which 3 were waited for; matrix products, arithmetic and copies ran while one was open for 2% of the time, Pallas kernels for 0%

profile of v1, /device:TPU:0, one launch (start us, length us, event | category | flops | bytes accessed | tf_op | source)
XLA Modules:
  0.0 209.9 jit_solution(7108358039005800175)
XLA Ops:
  6.5 0.0 copy-start
  6.5 0.0 slice-start
  6.5 0.0 slice-start.1
  6.5 0.0 all-gather.2.cloned.1.call-start
  6.5 0.7 all-gather.2.cloned.1.call-update
  7.3 0.0 all-reduce.2.cloned.1.call-start
  7.3 0.4 slice-done
  7.7 0.3 copy.30
  7.9 4.9 %collective-permute-start = (bf16[128,2,1024]{0,2,1:T(8,128)(2,1)S(1)}, bf16[128,2,1024]{0,2,1:T(8,128)(2,1)S(1)}, u32[]{:S(2)}, u32[]{:S(2)}) collective-permute-start(bf16[128,2,1024]{0,2,1:T(8,128)(2,1)S(1)} %copy.30), channel_id=1, source_target_pairs={{0,2},{2,4},{4,6},{6,8},{8,10},{10,12},{12,14},{1,3},{3,5},{5,7},{... | collective-permute-start | bytes 1572872 | tf_op jit(solution)/shard_map/ppermute | solution.py:27
  12.8 1.3 collective-permute-start.1
  14.1 0.0 slice-done.1
  14.2 0.2 copy.31
  14.4 0.2 fusion.4
  14.6 26.2 %collective-permute-done = bf16[128,2,1024]{0,2,1:T(8,128)(2,1)S(1)} collective-permute-done((bf16[128,2,1024]{0,2,1:T(8,128)(2,1)S(1)}, bf16[128,2,1024]{0,2,1:T(8,128)(2,1)S(1)}, u32[]{:S(2)}, u32[]{:S(2)}) %collective-permute-start) | collective-permute-done | bytes 524320 | tf_op jit(solution)/shard_map/ppermute | solution.py:27
  40.8 0.0 collective-permute-done.1
  40.8 0.2 pad_maximum_fusion
  41.0 0.2 fusion.8
  41.2 1.9 fusion.9
  43.1 1.8 convolution_convert_fusion
  44.9 50.4 %all-gather.2.cloned.1.call-done = bf16[2048,1024]{1,0:T(8,128)(2,1)} async-done(((bf16[256,1024]{1,0:T(8,128)(2,1)}), bf16[2048,1024]{1,0:T(8,128)(2,1)}) %all-gather.2.cloned.1.call-update) | async-done | bytes 4194320 | tf_op jit(solution)/shard_map/all_gather | solution.py:459
  95.3 0.0 copy-start.4
  95.3 0.0 copy-start.3
  95.3 4.8 %fusion.10 = f32[128,2048]{1,0:T(8,128)} fusion(bf16[128,1024]{0,1:T(8,128)(2,1)S(1)} %bitcast.30, bf16[2048,1024]{1,0:T(8,128)(2,1)} %all-gather.2.cloned.1.call-done), kind=kOutput, calls=%fused_computation.31 | convolution fusion | flops 536870912 | bytes 5505024 | tf_op jit(solution)/shard_map/dot_general | solution.py:457
  100.0 0.0 all-reduce.2.cloned.1.call-update
  100.1 0.0 copy-done.4
  100.1 18.1 %all-reduce.2.cloned.1.call-done = f32[128,2048]{1,0:T(8,128)} async-done(((f32[128,2048]{1,0:T(8,128)}), f32[128,2048]{1,0:T(8,128)}) %all-reduce.2.cloned.1.call-update) | async-done | bytes 1048592 | tf_op jit(solution)/shard_map/psum | solution.py:463
  118.2 0.0 copy-done.3
  118.2 1.5 multiply_reduce_fusion
  119.7 0.0 copy-start.1
  119.7 0.0 copy-start.5
  119.7 0.9 copy-done.1
  120.6 0.2 add_convert_fusion.normed
  120.8 0.0 copy-done
  120.9 0.0 copy-start.2
  120.9 0.3 fusion.11
  121.2 0.0 copy-done.5
  121.2 0.6 select_reduce_fusion
  121.9 0.0 copy-done.2
  121.9 79.5 %shard_map.82 = bf16[128,1024]{1,0:T(8,128)(2,1)} custom-call(bf16[128,2048]{1,0:T(8,128)(2,1)} %copy-done.2, f32[64,128]{1,0:T(8,128)} %bitcast.31, f32[128,2048]{1,0:T(8,128)} %copy-done.1, f32[4,2048]{1,0:T(4,128)} %modulation.1, bf16[16,2,192,2048]{3,2,1,0:T(8,128)(2,1)} %bitcast.26, bf16[16,384,1024]{2,1,0:T(8,128)(2,1)} %down.1), custom_call_target="tpu_custom_call" | custom-call | tf_op jit(solution)/shard_map/pallas_call | solution.py:403
  201.4 1.7 copy.34
  (7 shorter events, 0.1 us)
Async XLA Ops:
  6.5 114.3 %copy-start = (bf16[2048,64]{0,1:T(8,128)(2,1)S(1)}, bf16[2048,64]{0,1:T(8,128)(2,1)}, u32[]{:S(2)}) copy-start(bf16[2048,64]{0,1:T(8,128)(2,1)} %param.12) | copy-start | bytes 786436
  6.5 1.1 slice-start
  6.5 7.6 %slice-start.1 = ((bf16[128,3,1024]{2,0,1:T(8,128)(2,1)}), bf16[128,1,1024]{2,0,1:T(8,128)(2,1)S(1)}, s32[]{:S(2)}) async-start(bf16[128,3,1024]{2,0,1:T(8,128)(2,1)} %param.9), calls=%async_computation.3 | async-start | bytes 524288 | tf_op jit(solution)/shard_map/slice | solution.py:451
  6.5 88.7 %all-gather.2.cloned.1.call-start = ((), (), s32[]{:S(2)}) async-start(), calls=%async_computation | async-start | bytes 4718592 | tf_op jit(solution)/shard_map/all_gather | solution.py:459
  7.3 110.9 %all-reduce.2.cloned.1.call-start = ((), (), s32[]{:S(2)}) async-start(), calls=%async_computation.1 | async-start | bytes 2097152 | tf_op jit(solution)/shard_map/psum | solution.py:463
  7.9 32.9 %collective-permute-start = (bf16[128,2,1024]{0,2,1:T(8,128)(2,1)S(1)}, bf16[128,2,1024]{0,2,1:T(8,128)(2,1)S(1)}, u32[]{:S(2)}, u32[]{:S(2)}) collective-permute-start(bf16[128,2,1024]{0,2,1:T(8,128)(2,1)S(1)} %copy.30), channel_id=1, source_target_pairs={{0,2},{2,4},{4,6},{6,8},{8,10},{10,12},{12,14},{1,3},{3,5},{5,7},{... | collective-permute-start | bytes 1572872 | tf_op jit(solution)/shard_map/ppermute | solution.py:27
  12.8 28.0 %collective-permute-start.1 = (bf16[128,2,1024]{0,2,1:T(8,128)(2,1)S(1)}, bf16[128,2,1024]{0,2,1:T(8,128)(2,1)S(1)}, u32[]{:S(2)}, u32[]{:S(2)}) collective-permute-start(bf16[128,2,1024]{0,2,1:T(8,128)(2,1)S(1)} %copy.30), channel_id=1, source_target_pairs={{2,0},{4,2},{6,4},{8,6},{10,8},{12,10},{14,12},{3,1},{5,3},{7,5},{... | collective-permute-start | bytes 1572872 | tf_op jit(solution)/shard_map/ppermute | solution.py:29
  95.3 4.8 %copy-start.4 = (f32[4,2048]{1,0:T(4,128)S(1)}, f32[4,2048]{1,0:T(4,128)}, u32[]{:S(2)}) copy-start(f32[4,2048]{1,0:T(4,128)} %modulation.1) | copy-start | bytes 98308
  95.3 22.9 %copy-start.3 = (bf16[128,2048]{1,0:T(8,128)(2,1)S(1)}, bf16[128,2048]{1,0:T(8,128)(2,1)}, u32[]{:S(2)}) copy-start(bf16[128,2048]{1,0:T(8,128)(2,1)} %param.8) | copy-start | bytes 1572868
  119.7 1.0 copy-start.1
  119.7 1.5 copy-start.5
  120.9 1.0 copy-start.2
Sparse Core Ops, SparseCore 0:
  9.5 85.7 all-gather.1
  100.2 17.9 all-reduce.1

commit v2 on v1

--- a/solution.py
+++ b/solution.py
@@ -72,7 +72,7 @@
 
 
 def expert_kernel(
-    rows_of, devices,
+    devices,
     normed, meta, state, modulation, gate_up, down,
     out,
     tok, disp, gu, dn, hid_own, hid_other, got_meta, pick, slot_gate, got_x, got_up, got_down, acc,
@@ -385,7 +385,294 @@
     lax.fori_loop(0, halves, hid_drain, 0)
 
 
-def expert_call(normed, gates, expert_ids, state, modulation, gate_up_weight, down_weight, experts):
+def front_kernel(
+    devices,
+    tokens, packed, weight, modulation, router, ids,
+    normed, state, meta,
+    near, wide, mixed, mine_out, their_out,
+    near_s, near_r, far_s, far_r, ag_s, ag_r, y_r, sum_s, sum_r,
+):
+    me = lax.axis_index("dev")
+    part = lax.axis_index("sub")
+    group = lax.axis_index("groups")
+    z = me // COLS
+    x = me % COLS
+    across = z * COLS + (1 - x)
+    lines = devices // COLS
+    count, width = tokens.shape
+    shard = weight.shape[0] // 2
+    not_top = z < lines - 1
+    not_bottom = z > 0
+    up_to = {"dev": jnp.minimum(me + COLS, devices - 1)}
+    down_to = {"dev": jnp.maximum(me - COLS, 0)}
+    x_to = {"dev": across}
+    y_to = {"groups": 1 - group}
+    core_to = {"sub": 1 - part}
+
+    barrier = pltpu.get_barrier_semaphore()
+    for step in range(1, devices):
+        pl.semaphore_signal(
+            barrier, inc=1, device_id={"dev": (me + step) % devices}, device_id_type=MESH
+        )
+    pl.semaphore_signal(barrier, inc=1, device_id=core_to, device_id_type=MESH)
+    pl.semaphore_signal(barrier, inc=1, device_id=y_to, device_id_type=MESH)
+    pl.semaphore_wait(barrier, devices + 1)
+
+    def remote(src, dst, send, recv, where):
+        return pltpu.make_async_remote_copy(
+            src_ref=src, dst_ref=dst, send_sem=send, recv_sem=recv,
+            device_id=where, device_id_type=MESH,
+        )
+
+    def near_copy(i):
+        return remote(packed.at[1 + i], near.at[x, i], near_s.at[i], near_r.at[i], x_to)
+
+    def far_copy(i, where):
+        return remote(near.at[1 - x, i], near.at[x, i], far_s.at[i], far_r.at[i], where)
+
+    def piece(s, way, where, src=None):
+        dst = wide.at[s, group]
+        recv = y_r.at[s] if way == 3 else ag_r.at[s]
+        return remote(dst if src is None else src, dst, ag_s.at[s, way], recv, where)
+
+    far_up = (x == 0) & not_top
+    far_down = (x == 1) & not_bottom
+    have_far = ((x == 0) & not_bottom) | ((x == 1) & not_top)
+    mine = weight.at[pl.ds(pl.multiple_of(group * shard, SLOT), shard)]
+
+    for i in range(2):
+        near_copy(i).start()
+
+    @pl.when(not_top)
+    def _():
+        piece(me, 0, up_to, mine).start()
+
+    @pl.when(not_bottom)
+    def _():
+        piece(me, 1, down_to, mine).start()
+
+    piece(me, 2, x_to, mine).start()
+
+    @pl.when(jnp.logical_not(have_far))
+    def _():
+        near[x] = jnp.zeros_like(near[x])
+
+    for i in range(2):
+        near_copy(i).wait_recv()
+
+        @pl.when(far_up)
+        def _():
+            far_copy(i, up_to).start()
+
+        @pl.when(far_down)
+        def _():
+            far_copy(i, down_to).start()
+
+    def both(d, act):
+        @pl.when(z - d >= 0)
+        def _():
+            act(z - d, True)
+
+        @pl.when(z + d < lines)
+        def _():
+            act(z + d, False)
+
+    def project(s, rows, block):
+        mine_out[s, rows] = lax.dot_general(
+            mixed[...], block, (((1,), (1,)), ((), ())), preferred_element_type=jnp.float32
+        )
+        sum_copy(s, rows).start()
+
+    def sum_copy(s, rows):
+        return remote(
+            mine_out.at[s, rows], their_out.at[s, rows], sum_s.at[s, rows], sum_r.at[s, rows], core_to
+        )
+
+    def take_line(zz, low):
+        s = zz * COLS + x
+        piece(s, 2, x_to).wait_recv()
+
+        @pl.when(not_top if low else not_bottom)
+        def _():
+            piece(s, 0 if low else 1, up_to if low else down_to).start()
+
+        piece(s, 2, x_to).start()
+        piece(s, 3, y_to).start()
+
+    def take_across(zz, low):
+        s = zz * COLS + (1 - x)
+        piece(s, 2, x_to).wait_recv()
+        piece(s, 3, y_to).start()
+
+    def take_y(s):
+        dst = wide.at[s, 1 - group]
+        remote(dst, dst, ag_s.at[s, 3], y_r.at[s], y_to).wait_recv()
+        project(s, 1 - group, wide[s, 1 - group])
+
+    def use(s):
+        project(s, group, wide[s, group])
+
+    both(1, take_line)
+    take_across(z, False)
+
+    @pl.when(have_far)
+    def _():
+        for i in range(2):
+            far_copy(i, x_to).wait_recv()
+
+    row = lax.broadcasted_iota(jnp.int32, (count, count), 0)
+    col = lax.broadcasted_iota(jnp.int32, (count, count), 1)
+    see_before = (col >= row) & (me > 0)
+    see_after = (col <= row) & (me < devices - 1)
+    for h in range(mixed.shape[1] // HEAD):
+        lanes = slice(h * HEAD, (h + 1) * HEAD)
+        query = packed[0, :, lanes]
+
+        def score(keys):
+            return lax.dot_general(
+                query, keys, (((1,), (1,)), ((), ())), preferred_element_type=jnp.float32
+            ) / math.sqrt(HEAD)
+
+        scores = jnp.concatenate(
+            [
+                jnp.where(see_before, score(near[0, 0, :, lanes]), NEG),
+                score(packed[1, :, lanes]),
+                jnp.where(see_after, score(near[1, 0, :, lanes]), NEG),
+            ],
+            axis=1,
+        )
+        top = jnp.max(scores, -1, keepdims=True)
+        share = jnp.exp(scores - top)
+        share = (share / jnp.sum(share, -1, keepdims=True)).astype(jnp.bfloat16)
+        values = jnp.concatenate(
+            [near[0, 1, :, lanes], packed[2, :, lanes], near[1, 1, :, lanes]], axis=0
+        )
+        mixed[:, lanes] = jnp.dot(
+            share, values, preferred_element_type=jnp.float32
+        ).astype(jnp.bfloat16)
+
+    for rows in range(2):
+        project(me, rows, weight[rows * shard:(rows + 1) * shard])
+    both(1, lambda zz, low: use(zz * COLS + x))
+    use(across)
+    for d in range(2, lines):
+        both(d, take_line)
+        both(d - 1, lambda zz, low: take_y(zz * COLS + x))
+        if d == 2:
+            take_y(across)
+        both(d, lambda zz, low: use(zz * COLS + x))
+    if lines > 1:
+        both(lines - 1, lambda zz, low: take_y(zz * COLS + x))
+    if lines < 3:
+        take_y(across)
+    for d in range(1, lines):
+        both(d, take_across)
+        both(d, lambda zz, low: use(zz * COLS + (1 - x)))
+        if d > 1:
+            both(d - 1, lambda zz, low: take_y(zz * COLS + (1 - x)))
+    if lines > 1:
+        both(lines - 1, lambda zz, low: take_y(zz * COLS + (1 - x)))
+
+    square = jnp.zeros((count, 1), jnp.float32)
+    for s in range(devices):
+        for rows in range(2):
+            sum_copy(s, rows).wait_recv()
+            at = (2 * s + rows) * shard
+            lanes = slice(at, at + shard)
+            value = tokens[:, lanes].astype(jnp.float32) + (1.0 + modulation[0:1, lanes]) * (
+                mine_out[s, rows] + their_out[s, rows]
+            )
+            state[:, lanes] = value
+            square = square + jnp.sum(value * value, -1, keepdims=True)
+    scale = lax.rsqrt(square / width + EPS)
+    for s in range(2 * devices):
+        lanes = slice(s * shard, (s + 1) * shard)
+        normed[:, lanes] = (
+            state[:, lanes] * scale * (1.0 + modulation[2:3, lanes]) + modulation[1:2, lanes]
+        ).astype(jnp.bfloat16)
+    logits = lax.dot_general(
+        router[...], normed[...], (((1,), (1,)), ((), ())), preferred_element_type=jnp.float32
+    )
+    name = lax.broadcasted_iota(jnp.int32, logits.shape, 0)
+    named = name == ids[0:1]
+    for k in range(1, ids.shape[0]):
+        named = named | (name == ids[k:k + 1])
+    lifted = jnp.where(named, jax.nn.sigmoid(logits), 0.0)
+    meta[...] = lifted / jnp.sum(lifted, 0, keepdims=True)
+
+    for i in range(2):
+        near_copy(i).wait_send()
+
+        @pl.when(far_up | far_down)
+        def _():
+            far_copy(i, x_to).wait_send()
+
+    @pl.when(not_top)
+    def _():
+        piece(me, 0, up_to, mine).wait_send()
+
+    @pl.when(not_bottom)
+    def _():
+        piece(me, 1, down_to, mine).wait_send()
+
+    piece(me, 2, x_to, mine).wait_send()
+    piece(across, 3, y_to).wait_send()
+    for d in range(1, lines):
+
+        def sent(zz, low):
+            s = zz * COLS + x
+
+            @pl.when(not_top if low else not_bottom)
+            def _():
+                piece(s, 0 if low else 1, up_to).wait_send()
+
+            piece(s, 2, x_to).wait_send()
+            piece(s, 3, y_to).wait_send()
+            piece(zz * COLS + (1 - x), 3, y_to).wait_send()
+
+        both(d, sent)
+    for s in range(devices):
+        for rows in range(2):
+            sum_copy(s, rows).wait_send()
+
+
+def front_call(tokens, query_key_value, out_weight, modulation, router_weight, expert_ids):
+    devices = lax.axis_size("dev")
+    count, width = tokens.shape
+    local = query_key_value.shape[2]
+    shard = out_weight.shape[0] // 2
+    lines = devices // COLS
+    vmem = pl.BlockSpec(memory_space=pltpu.VMEM)
+    dma = pltpu.SemaphoreType.DMA
+    return pl.pallas_call(
+        functools.partial(front_kernel, devices),
+        out_shape=(
+            jax.ShapeDtypeStruct((count, width), jnp.bfloat16),
+            jax.ShapeDtypeStruct((count, width), jnp.float32),
+            jax.ShapeDtypeStruct((router_weight.shape[1], count), jnp.float32),
+        ),
+        in_specs=[vmem] * 6,
+        out_specs=(vmem, vmem, vmem),
+        scratch_shapes=[
+            pltpu.VMEM((2, 2, count, local), jnp.bfloat16),
+            pltpu.VMEM((devices, 2, shard, local), jnp.bfloat16),
+            pltpu.VMEM((count, local), jnp.bfloat16),
+            pltpu.VMEM((devices, 2, count, shard), jnp.float32),
+            pltpu.VMEM((devices, 2, count, shard), jnp.float32),
+            dma((2,)), dma((2,)), dma((2,)), dma((2,)),
+            dma((devices, 4)), dma((devices,)), dma((devices,)),
+            dma((devices, 2)), dma((devices, 2)),
+        ],
+        compiler_params=pltpu.CompilerParams(
+            collective_id=2, has_side_effects=True, vmem_limit_bytes=VMEM_BYTES // 2
+        ),
+    )(
+        tokens, query_key_value.transpose(1, 0, 2), out_weight, modulation,
+        router_weight.T, expert_ids.T,
+    )
+
+
+def expert_call(normed, meta, state, modulation, gate_up_weight, down_weight):
     devices = lax.axis_size("dev")
     count, width = normed.shape
     half = down_weight.shape[2]
@@ -395,13 +682,11 @@
     hidden = gate_up_weight.shape[2]
     lines = devices // COLS
     rows = devices * SLOT
-    match = expert_ids[:, None, :] == jnp.arange(experts, dtype=jnp.int32)[None, :, None]
-    meta = jnp.sum(jnp.where(match, gates[:, None, :], 0.0), -1).T
     vmem = pl.BlockSpec(memory_space=pltpu.VMEM)
     hbm = pl.BlockSpec(memory_space=pl.ANY)
     dma = pltpu.SemaphoreType.DMA
     return pl.pallas_call(
-        functools.partial(expert_kernel, rows, devices),
+        functools.partial(expert_kernel, devices),
         out_shape=jax.ShapeDtypeStruct((count, half), jnp.bfloat16),
         in_specs=[vmem, vmem, vmem, vmem, hbm, hbm],
         out_specs=vmem,
@@ -447,6 +732,16 @@
     devices = lax.axis_size("dev")
     total = count * devices
     local_width = query_key_value.shape[2]
+    weight_bytes = 2 * (gate_up_weight.size + down_weight.size)
+    token_bytes = 10 * devices * count * width
+    fits = weight_bytes + token_bytes < VMEM_BYTES and CAP <= SLOT
+    paired = parts == 2 and lax.axis_size("groups") == 2 and devices % COLS == 0
+    tiled = out_weight.shape[0] % (2 * LANES) == 0 and count == LANES
+    if fits and paired and tiled:
+        normed, state, meta = front_call(
+            tokens, query_key_value, out_weight, modulation, router_weight, expert_ids
+        )
+        return expert_call(normed, meta, state, modulation, gate_up_weight, down_weight)
     heads_here = local_width // HEAD
     query = query_key_value[:, 0].reshape(count, heads_here, HEAD)
     pair = query_key_value[:, 1:]
@@ -465,12 +760,6 @@
     normed = normalize(state, modulation)
     gates = route(normed, router_weight, expert_ids)
     experts = router_weight.shape[1]
-    weight_bytes = 2 * (gate_up_weight.size + down_weight.size)
-    token_bytes = 10 * devices * count * width
-    if devices % COLS == 0 and parts == 2 and weight_bytes + token_bytes < VMEM_BYTES:
-        return expert_call(
-            normed, gates, expert_ids, state, modulation, gate_up_weight, down_weight, experts
-        )
     topk = expert_ids.shape[1]
     flat = expert_ids.reshape(-1)
     picks = flat.shape[0]

time: 210 us -> 152 us (0.72)
  waiting for transfers between devices: 95.5 us -> 0 us
  Pallas kernels: 79.5 us -> 142 us
  between operations: 13.6 us -> 0.03 us
  matrix products: 8.72 us -> 0 us
  starting transfers between devices: 6.24 us -> 0 us
  local copies, waits for them, and re-layouts: 3.59 us -> 9.66 us
  other arithmetic: 2.85 us -> 0 us
    pallas_call x1 -> x2, Pallas kernels: 79.5 us -> 142 us  [the longest x1 79.9 us: expert_call(): pl.pallas_call(functools.partial(expert_kernel, devices), out_shape=jax.S...]
    all_gather x1 -> x0, waiting for transfers between devices: 50.4 us -> none  [body(): lax.all_gather(out_weight, 'dev', axis=0, tiled=True)]
    ppermute x2 -> x0, waiting for transfers between devices: 26.2 us -> none  [the longest x1 26.2 us: extended(): lax.ppermute(tail, axis, [(i, (i + 1) % count) for i in range(ends)])]
    psum x1 -> x0, waiting for transfers between devices: 18.1 us -> none  [body(): proj = lax.psum(partial_proj, 'sub')]
    dot_general x3 -> x0, matrix products: 6.84 us -> none  [the longest x1 4.75 us: body(): lax.dot_general(mixed, lax.all_gather(out_weight, 'dev', axis=0, tiled=Tr...]
    unnamed x15 -> x19, local copies, waits for them, and re-layouts: 3.08 us -> 9.66 us
    ppermute x2 -> x0, starting transfers between devices: 6.2 us -> none  [the longest x1 4.9 us: extended(): lax.ppermute(tail, axis, [(i, (i + 1) % count) for i in range(ends)])]
    reduce_sum x4 -> x0, other arithmetic: 2.19 us -> none  [the longest x1 1.48 us: normalize(): scale = lax.rsqrt(jnp.mean(state * state, -1, keepdims=True) + EPS)]
  transfers between devices with their start and end apart: 4 -> 0, of which waited for: 3 -> 0; matrix products, arithmetic and copies ran while one was open for 2% -> 0% of each run, Pallas kernels for 0% -> 0%
where the time goes in v2:
time: 152 us
  Pallas kernels  142 us (93%)
  local copies, waits for them, and re-layouts  9.66 us (6%)
    pallas_call x1, Pallas kernels, expert_call(): pl.pallas_call(functools.partial(expert_kernel, devices), out_shape=jax.S...  79.9 us
    pallas_call x1, Pallas kernels, front_call(): pl.pallas_call(functools.partial(front_kernel, devices), out_shape=(jax.S...  62.1 us
    unnamed x19, local copies, waits for them, and re-layouts  9.66 us

profile of v2, /device:TPU:0, one launch (start us, length us, event | category | flops | bytes accessed | tf_op | source)
XLA Modules:
  0.0 151.7 jit_solution(15186508765304675860)
XLA Ops:
  0.0 0.0 copy-start.1
  0.0 1.1 copy-done.1
  1.1 0.0 copy-start.3
  1.1 1.0 copy-done.3
  2.2 0.0 copy-start.4
  2.2 1.0 copy-done.4
  3.2 0.0 copy-start.5
  3.2 0.9 copy-done.5
  4.2 0.0 copy-start.6
  4.2 0.8 copy-done.6
  4.9 0.0 copy-start.8
  4.9 0.7 copy-done.8
  5.6 62.1 %shard_map.82 = (bf16[128,2048]{1,0:T(8,128)(2,1)S(1)}, f32[128,2048]{1,0:T(8,128)S(1)}, f32[64,128]{1,0:T(8,128)S(1)}) custom-call(bf16[128,2048]{1,0:T(8,128)(2,1)S(1)} %copy-done.3, bf16[3,128,1024]{2,1,0:T(8,128)(2,1)S(1)} %bitcast.4, bf16[256,1024]{1,0:T(8,128)(2,1)S(1)} %copy-done.4, f32[4,2048]{1,0:T(4,128)S(1)} %copy-done.6, ...), custom_call_target="tpu_custom_call" | custom-call | tf_op jit(solution)/shard_map/pallas_call | solution.py:647
  67.7 0.0 copy-start
  67.7 1.0 copy-done
  68.7 0.0 copy-start.2
  68.7 0.8 copy-done.2
  69.5 0.0 copy-start.7
  69.5 0.6 copy-done.7
  70.1 79.9 %shard_map.83 = bf16[128,1024]{1,0:T(8,128)(2,1)} custom-call(bf16[128,2048]{1,0:T(8,128)(2,1)} %copy-done.2, f32[64,128]{1,0:T(8,128)} %copy-done.7, f32[128,2048]{1,0:T(8,128)} %copy-done, f32[4,2048]{1,0:T(4,128)} %modulation.3, bf16[16,2,192,2048]{3,2,1,0:T(8,128)(2,1)} %bitcast.7, bf16[16,384,1024]{2,1,0:T(8,128)(2,1)} %down.1), custom_call_target="tpu_custom_call" | custom-call | tf_op jit(solution)/shard_map/pallas_call | solution.py:688
  150.1 1.7 %copy.10 = bf16[128,1024]{1,0:T(8,128)(2,1)} copy(bf16[128,1024]{1,0:T(8,128)(2,1)} %shard_map.83) | data formatting | bytes 524288
Async XLA Ops:
  0.0 1.1 copy-start.1
  1.1 1.0 copy-start.3
  2.2 1.0 copy-start.4
  3.2 0.9 copy-start.5
  4.2 0.8 copy-start.6
  4.9 0.7 copy-start.8
  67.7 1.0 copy-start
  68.7 0.8 copy-start.2
  69.5 0.6 copy-start.7

commit v3 on v2

--- a/solution.py
+++ b/solution.py
@@ -72,11 +72,11 @@
 
 
 def expert_kernel(
-    devices,
+    devices, weight_copies,
     normed, meta, state, modulation, gate_up, down,
     out,
     tok, disp, gu, dn, hid_own, hid_other, got_meta, pick, slot_gate, got_x, got_up, got_down, acc,
-    meta_s, meta_r, ag_s, ag_r, core_r, gu_sem, dn_sem, hid_s, hid_r,
+    meta_s, meta_r, ag_s, ag_r, core_r, hid_s, hid_r,
     x_s, x_r, up_s, up_r, down_s, down_r,
 ):
     me = lax.axis_index("dev")
@@ -93,20 +93,6 @@
     hidden = gate_up.shape[2]
     slots = local * SLOT
 
-    def weight_copies(h):
-        return (
-            pltpu.make_async_copy(gate_up.at[h], gu.at[h], gu_sem.at[h]),
-            pltpu.make_async_copy(down.at[h], dn.at[h], dn_sem.at[h]),
-        )
-
-    barrier = pltpu.get_barrier_semaphore()
-    for step in range(1, devices):
-        pl.semaphore_signal(
-            barrier, inc=1, device_id={"dev": (me + step) % devices}, device_id_type=MESH
-        )
-    pl.semaphore_signal(barrier, inc=1, device_id={"sub": other}, device_id_type=MESH)
-    pl.semaphore_wait(barrier, devices)
-
     def remote(src, dst, send, recv, where):
         return pltpu.make_async_remote_copy(
             src_ref=src, dst_ref=dst, send_sem=send, recv_sem=recv,
@@ -145,13 +131,6 @@
         block(me, 1, down_to, mine).start()
 
     block(me, 2, x_to, mine).start()
-
-    def start_weights(h, carry):
-        for copy in weight_copies(h):
-            copy.start()
-        return carry
-
-    lax.fori_loop(0, halves, start_weights, 0)
 
     before = (
         lax.broadcasted_iota(jnp.int32, (count, count), 0)
@@ -386,12 +365,20 @@
 
 
 def front_kernel(
-    devices,
-    tokens, packed, weight, modulation, router, ids,
+    devices, start_weights,
+    sources, held, own_sem,
     normed, state, meta,
     near, wide, mixed, mine_out, their_out,
     near_s, near_r, far_s, far_r, ag_s, ag_r, y_r, sum_s, sum_r,
 ):
+    packed_hbm, weight_hbm = sources[1], sources[2]
+    tokens, packed, weight, modulation, router, ids = held
+
+    def own_copy(i):
+        return pltpu.make_async_copy(sources[i], held[i], own_sem.at[i])
+
+    for i in (1, 2, 0, 3, 4, 5):
+        own_copy(i).start()
     me = lax.axis_index("dev")
     part = lax.axis_index("sub")
     group = lax.axis_index("groups")
@@ -425,7 +412,7 @@
         )
 
     def near_copy(i):
-        return remote(packed.at[1 + i], near.at[x, i], near_s.at[i], near_r.at[i], x_to)
+        return remote(packed_hbm.at[1 + i], near.at[x, i], near_s.at[i], near_r.at[i], x_to)
 
     def far_copy(i, where):
         return remote(near.at[1 - x, i], near.at[x, i], far_s.at[i], far_r.at[i], where)
@@ -438,7 +425,7 @@
     far_up = (x == 0) & not_top
     far_down = (x == 1) & not_bottom
     have_far = ((x == 0) & not_bottom) | ((x == 1) & not_top)
-    mine = weight.at[pl.ds(pl.multiple_of(group * shard, SLOT), shard)]
+    mine = weight_hbm.at[pl.ds(pl.multiple_of(group * shard, SLOT), shard)]
 
     for i in range(2):
         near_copy(i).start()
@@ -452,6 +439,7 @@
         piece(me, 1, down_to, mine).start()
 
     piece(me, 2, x_to, mine).start()
+    start_weights()
 
     @pl.when(jnp.logical_not(have_far))
     def _():
@@ -514,6 +502,8 @@
 
     both(1, take_line)
     take_across(z, False)
+    for i in range(6):
+        own_copy(i).wait()
 
     @pl.when(have_far)
     def _():
@@ -636,45 +626,45 @@
             sum_copy(s, rows).wait_send()
 
 
-def front_call(tokens, query_key_value, out_weight, modulation, router_weight, expert_ids):
+def block_kernel(devices, *refs):
+    sources, gate_up, down, out = refs[:6], refs[6], refs[7], refs[8]
+    held, normed, state, meta = refs[9:15], refs[15], refs[16], refs[17]
+    front_buffers, expert_buffers = refs[18:23], refs[23:36]
+    own_sem, gu_sem, dn_sem = refs[36:39]
+    front_sems, expert_sems = refs[39:48], refs[48:]
+    gu, dn = expert_buffers[2:4]
+    halves = gate_up.shape[0]
+
+    def weight_copies(h):
+        return (
+            pltpu.make_async_copy(gate_up.at[h], gu.at[h], gu_sem.at[h]),
+            pltpu.make_async_copy(down.at[h], dn.at[h], dn_sem.at[h]),
+        )
+
+    def start_weights():
+        def one(h, carry):
+            for copy in weight_copies(h):
+                copy.start()
+            return carry
+
+        lax.fori_loop(0, halves, one, 0)
+
+    front_kernel(
+        devices, start_weights, sources, held, own_sem, normed, state, meta,
+        *front_buffers, *front_sems,
+    )
+    expert_kernel(
+        devices, weight_copies, normed, meta, state, held[3], gate_up, down, out,
+        *expert_buffers, *expert_sems,
+    )
+
+
+def block_call(
+    tokens, query_key_value, out_weight, modulation, router_weight, expert_ids,
+    gate_up_weight, down_weight,
+):
     devices = lax.axis_size("dev")
     count, width = tokens.shape
-    local = query_key_value.shape[2]
-    shard = out_weight.shape[0] // 2
-    lines = devices // COLS
-    vmem = pl.BlockSpec(memory_space=pltpu.VMEM)
-    dma = pltpu.SemaphoreType.DMA
-    return pl.pallas_call(
-        functools.partial(front_kernel, devices),
-        out_shape=(
-            jax.ShapeDtypeStruct((count, width), jnp.bfloat16),
-            jax.ShapeDtypeStruct((count, width), jnp.float32),
-            jax.ShapeDtypeStruct((router_weight.shape[1], count), jnp.float32),
-        ),
-        in_specs=[vmem] * 6,
-        out_specs=(vmem, vmem, vmem),
-        scratch_shapes=[
-            pltpu.VMEM((2, 2, count, local), jnp.bfloat16),
-            pltpu.VMEM((devices, 2, shard, local), jnp.bfloat16),
-            pltpu.VMEM((count, local), jnp.bfloat16),
-            pltpu.VMEM((devices, 2, count, shard), jnp.float32),
-            pltpu.VMEM((devices, 2, count, shard), jnp.float32),
-            dma((2,)), dma((2,)), dma((2,)), dma((2,)),
-            dma((devices, 4)), dma((devices,)), dma((devices,)),
-            dma((devices, 2)), dma((devices, 2)),
-        ],
-        compiler_params=pltpu.CompilerParams(
-            collective_id=2, has_side_effects=True, vmem_limit_bytes=VMEM_BYTES // 2
-        ),
-    )(
-        tokens, query_key_value.transpose(1, 0, 2), out_weight, modulation,
-        router_weight.T, expert_ids.T,
-    )
-
-
-def expert_call(normed, meta, state, modulation, gate_up_weight, down_weight):
-    devices = lax.axis_size("dev")
-    count, width = normed.shape
     half = down_weight.shape[2]
     halves = gate_up_weight.shape[0]
     local = halves // 2
@@ -682,15 +672,28 @@
     hidden = gate_up_weight.shape[2]
     lines = devices // COLS
     rows = devices * SLOT
-    vmem = pl.BlockSpec(memory_space=pltpu.VMEM)
+    shard = out_weight.shape[0] // 2
+    own = (
+        tokens, query_key_value.transpose(1, 0, 2), out_weight, modulation,
+        router_weight.T, expert_ids.T,
+    )
     hbm = pl.BlockSpec(memory_space=pl.ANY)
     dma = pltpu.SemaphoreType.DMA
     return pl.pallas_call(
-        functools.partial(expert_kernel, devices),
+        functools.partial(block_kernel, devices),
         out_shape=jax.ShapeDtypeStruct((count, half), jnp.bfloat16),
-        in_specs=[vmem, vmem, vmem, vmem, hbm, hbm],
-        out_specs=vmem,
+        in_specs=[hbm] * 8,
+        out_specs=pl.BlockSpec(memory_space=pltpu.VMEM),
         scratch_shapes=[
+            *[pltpu.VMEM(array.shape, array.dtype) for array in own],
+            pltpu.VMEM((count, width), jnp.bfloat16),
+            pltpu.VMEM((count, width), jnp.float32),
+            pltpu.VMEM((router_weight.shape[1], count), jnp.float32),
+            pltpu.VMEM((2, 2, count, half), jnp.bfloat16),
+            pltpu.VMEM((devices, 2, shard, half), jnp.bfloat16),
+            pltpu.VMEM((count, half), jnp.bfloat16),
+            pltpu.VMEM((devices, 2, count, shard), jnp.float32),
+            pltpu.VMEM((devices, 2, count, shard), jnp.float32),
             pltpu.VMEM((2, devices, count, half), jnp.bfloat16),
             pltpu.VMEM((2, local, rows, half), jnp.bfloat16),
             pltpu.VMEM(gate_up_weight.shape, jnp.bfloat16),
@@ -704,14 +707,18 @@
             pltpu.VMEM((lines, count, half), jnp.bfloat16),
             pltpu.VMEM((lines, count, half), jnp.bfloat16),
             pltpu.VMEM((count, half), jnp.float32),
+            dma((6,)), dma((halves,)), dma((halves,)),
+            dma((2,)), dma((2,)), dma((2,)), dma((2,)),
+            dma((devices, 4)), dma((devices,)), dma((devices,)),
+            dma((devices, 2)), dma((devices, 2)),
             dma((devices,)), dma((devices,)), dma((devices, 4)), dma((devices,)), dma((devices,)),
-            dma((halves,)), dma((halves,)), dma((halves,)), dma((halves,)),
+            dma((halves,)), dma((halves,)),
             dma((lines,)), dma((lines,)), dma((lines,)), dma((lines,)), dma((lines,)), dma((lines,)),
         ],
         compiler_params=pltpu.CompilerParams(
             collective_id=1, has_side_effects=True, vmem_limit_bytes=VMEM_BYTES
         ),
-    )(normed, meta, state, modulation, gate_up_weight, down_weight)
+    )(*own, gate_up_weight, down_weight)
 
 
 def body(
@@ -733,15 +740,15 @@
     total = count * devices
     local_width = query_key_value.shape[2]
     weight_bytes = 2 * (gate_up_weight.size + down_weight.size)
-    token_bytes = 10 * devices * count * width
+    token_bytes = 12 * devices * count * width
     fits = weight_bytes + token_bytes < VMEM_BYTES and CAP <= SLOT
     paired = parts == 2 and lax.axis_size("groups") == 2 and devices % COLS == 0
     tiled = out_weight.shape[0] % (2 * LANES) == 0 and count == LANES
     if fits and paired and tiled:
-        normed, state, meta = front_call(
-            tokens, query_key_value, out_weight, modulation, router_weight, expert_ids
-        )
-        return expert_call(normed, meta, state, modulation, gate_up_weight, down_weight)
+        return block_call(
+            tokens, query_key_value, out_weight, modulation, router_weight, expert_ids,
+            gate_up_weight, down_weight,
+        )
     heads_here = local_width // HEAD
     query = query_key_value[:, 0].reshape(count, heads_here, HEAD)
     pair = query_key_value[:, 1:]

time: 152 us -> 139 us (0.914)
  local copies, waits for them, and re-layouts: 9.66 us -> 1.67 us
  Pallas kernels: 142 us -> 137 us
    unnamed x19 -> x1, local copies, waits for them, and re-layouts: 9.66 us -> 1.67 us
    pallas_call x2 -> x1, Pallas kernels: 142 us -> 137 us  [block_call(): pl.pallas_call(functools.partial(block_kernel, devices), out_shape=jax.Sh...]
where the time goes in v3:
time: 139 us
  Pallas kernels  137 us (99%)
  local copies, waits for them, and re-layouts  1.67 us (1%)
    pallas_call x1, Pallas kernels, block_call(): pl.pallas_call(functools.partial(block_kernel, devices), out_shape=jax.Sh...  137 us

profile of v3, /device:TPU:0, one launch (start us, length us, event | category | flops | bytes accessed | tf_op | source)
XLA Modules:
  0.0 138.6 jit_solution(9746108848402728272)
XLA Ops:
  0.0 136.9 %shard_map.82 = bf16[128,1024]{1,0:T(8,128)(2,1)} custom-call(bf16[128,2048]{1,0:T(8,128)(2,1)} %refs_0_.1, bf16[3,128,1024]{2,1,0:T(8,128)(2,1)} %bitcast.5, bf16[256,1024]{1,0:T(8,128)(2,1)} %refs_2_.1, f32[4,2048]{1,0:T(4,128)} %refs_3_.1, bf16[64,2048]{1,0:T(8,128)(2,1)} %bitcast.6, s32[4,128]{1,0:T(4,128)} %bitcast.7, ...), custom_call_target="tpu_custom_call" | custom-call | tf_op jit(solution)/shard_map/pallas_call | solution.py:682
  137.0 1.7 %copy.10 = bf16[128,1024]{1,0:T(8,128)(2,1)} copy(bf16[128,1024]{1,0:T(8,128)(2,1)} %shard_map.82) | data formatting | bytes 524288

commit v4 on v3

--- a/solution.py
+++ b/solution.py
@@ -387,7 +387,9 @@
     across = z * COLS + (1 - x)
     lines = devices // COLS
     count, width = tokens.shape
-    shard = weight.shape[0] // 2
+    shard = weight.shape[0]
+    extra = shard * 3 // 8 // SLOT * SLOT
+    main = shard - extra
     not_top = z < lines - 1
     not_bottom = z > 0
     up_to = {"dev": jnp.minimum(me + COLS, devices - 1)}
@@ -418,14 +420,15 @@
         return remote(near.at[1 - x, i], near.at[x, i], far_s.at[i], far_r.at[i], where)
 
     def piece(s, way, where, src=None):
-        dst = wide.at[s, group]
+        start, size = (main, extra) if way == 3 else (extra, main)
+        dst = wide.at[s, pl.ds(pl.multiple_of(group * start, SLOT), size)]
         recv = y_r.at[s] if way == 3 else ag_r.at[s]
         return remote(dst if src is None else src, dst, ag_s.at[s, way], recv, where)
 
     far_up = (x == 0) & not_top
     far_down = (x == 1) & not_bottom
     have_far = ((x == 0) & not_bottom) | ((x == 1) & not_top)
-    mine = weight_hbm.at[pl.ds(pl.multiple_of(group * shard, SLOT), shard)]
+    mine = weight_hbm.at[pl.ds(pl.multiple_of(group * extra, SLOT), main)]
 
     for i in range(2):
         near_copy(i).start()
@@ -465,16 +468,14 @@
         def _():
             act(z + d, False)
 
-    def project(s, rows, block):
-        mine_out[s, rows] = lax.dot_general(
+    def project(s, block):
+        mine_out[s] = lax.dot_general(
             mixed[...], block, (((1,), (1,)), ((), ())), preferred_element_type=jnp.float32
         )
-        sum_copy(s, rows).start()
-
-    def sum_copy(s, rows):
-        return remote(
-            mine_out.at[s, rows], their_out.at[s, rows], sum_s.at[s, rows], sum_r.at[s, rows], core_to
-        )
+        sum_copy(s).start()
+
+    def sum_copy(s):
+        return remote(mine_out.at[s], their_out.at[s], sum_s.at[s], sum_r.at[s], core_to)
 
     def take_line(zz, low):
         s = zz * COLS + x
@@ -493,15 +494,20 @@
         piece(s, 3, y_to).start()
 
     def take_y(s):
-        dst = wide.at[s, 1 - group]
+        dst = wide.at[s, pl.ds(pl.multiple_of((1 - group) * main, SLOT), extra)]
         remote(dst, dst, ag_s.at[s, 3], y_r.at[s], y_to).wait_recv()
-        project(s, 1 - group, wide[s, 1 - group])
-
-    def use(s):
-        project(s, group, wide[s, group])
+        project(s, wide[s])
+
+    def line_y(zz, low):
+        take_y(zz * COLS + x)
+
+    def across_y(zz, low):
+        take_y(zz * COLS + (1 - x))
 
     both(1, take_line)
     take_across(z, False)
+    for d in range(2, min(3, lines)):
+        both(d, take_line)
     for i in range(6):
         own_copy(i).wait()
 
@@ -541,41 +547,28 @@
             share, values, preferred_element_type=jnp.float32
         ).astype(jnp.bfloat16)
 
-    for rows in range(2):
-        project(me, rows, weight[rows * shard:(rows + 1) * shard])
-    both(1, lambda zz, low: use(zz * COLS + x))
-    use(across)
-    for d in range(2, lines):
+    project(me, weight[...])
+    for d in range(3, lines):
         both(d, take_line)
-        both(d - 1, lambda zz, low: take_y(zz * COLS + x))
-        if d == 2:
+    for d in range(1, lines):
+        both(d, line_y)
+        both(d, take_across)
+        if d == 1:
             take_y(across)
-        both(d, lambda zz, low: use(zz * COLS + x))
-    if lines > 1:
-        both(lines - 1, lambda zz, low: take_y(zz * COLS + x))
-    if lines < 3:
-        take_y(across)
     for d in range(1, lines):
-        both(d, take_across)
-        both(d, lambda zz, low: use(zz * COLS + (1 - x)))
-        if d > 1:
-            both(d - 1, lambda zz, low: take_y(zz * COLS + (1 - x)))
-    if lines > 1:
-        both(lines - 1, lambda zz, low: take_y(zz * COLS + (1 - x)))
+        both(d, across_y)
 
     square = jnp.zeros((count, 1), jnp.float32)
     for s in range(devices):
-        for rows in range(2):
-            sum_copy(s, rows).wait_recv()
-            at = (2 * s + rows) * shard
-            lanes = slice(at, at + shard)
-            value = tokens[:, lanes].astype(jnp.float32) + (1.0 + modulation[0:1, lanes]) * (
-                mine_out[s, rows] + their_out[s, rows]
-            )
-            state[:, lanes] = value
-            square = square + jnp.sum(value * value, -1, keepdims=True)
+        sum_copy(s).wait_recv()
+        lanes = slice(s * shard, (s + 1) * shard)
+        value = tokens[:, lanes].astype(jnp.float32) + (1.0 + modulation[0:1, lanes]) * (
+            mine_out[s] + their_out[s]
+        )
+        state[:, lanes] = value
+        square = square + jnp.sum(value * value, -1, keepdims=True)
     scale = lax.rsqrt(square / width + EPS)
-    for s in range(2 * devices):
+    for s in range(devices):
         lanes = slice(s * shard, (s + 1) * shard)
         normed[:, lanes] = (
             state[:, lanes] * scale * (1.0 + modulation[2:3, lanes]) + modulation[1:2, lanes]
@@ -622,8 +615,7 @@
 
         both(d, sent)
     for s in range(devices):
-        for rows in range(2):
-            sum_copy(s, rows).wait_send()
+        sum_copy(s).wait_send()
 
 
 def block_kernel(devices, *refs):
@@ -672,7 +664,7 @@
     hidden = gate_up_weight.shape[2]
     lines = devices // COLS
     rows = devices * SLOT
-    shard = out_weight.shape[0] // 2
+    shard = out_weight.shape[0]
     own = (
         tokens, query_key_value.transpose(1, 0, 2), out_weight, modulation,
         router_weight.T, expert_ids.T,
@@ -690,10 +682,10 @@
             pltpu.VMEM((count, width), jnp.float32),
             pltpu.VMEM((router_weight.shape[1], count), jnp.float32),
             pltpu.VMEM((2, 2, count, half), jnp.bfloat16),
-            pltpu.VMEM((devices, 2, shard, half), jnp.bfloat16),
+            pltpu.VMEM((devices, shard, half), jnp.bfloat16),
             pltpu.VMEM((count, half), jnp.bfloat16),
-            pltpu.VMEM((devices, 2, count, shard), jnp.float32),
-            pltpu.VMEM((devices, 2, count, shard), jnp.float32),
+            pltpu.VMEM((devices, count, shard), jnp.float32),
+            pltpu.VMEM((devices, count, shard), jnp.float32),
             pltpu.VMEM((2, devices, count, half), jnp.bfloat16),
             pltpu.VMEM((2, local, rows, half), jnp.bfloat16),
             pltpu.VMEM(gate_up_weight.shape, jnp.bfloat16),
@@ -710,7 +702,7 @@
             dma((6,)), dma((halves,)), dma((halves,)),
             dma((2,)), dma((2,)), dma((2,)), dma((2,)),
             dma((devices, 4)), dma((devices,)), dma((devices,)),
-            dma((devices, 2)), dma((devices, 2)),
+            dma((devices,)), dma((devices,)),
             dma((devices,)), dma((devices,)), dma((devices, 4)), dma((devices,)), dma((devices,)),
             dma((halves,)), dma((halves,)),
             dma((lines,)), dma((lines,)), dma((lines,)), dma((lines,)), dma((lines,)), dma((lines,)),

time: 139 us -> 136 us (0.978)
  Pallas kernels: 137 us -> 134 us
    pallas_call x1, Pallas kernels: 137 us -> 134 us  [block_call(): pl.pallas_call(functools.partial(block_kernel, devices), out_shape=jax.Sh...]
where the time goes in v4:
time: 136 us
  Pallas kernels  134 us (99%)
  local copies, waits for them, and re-layouts  1.67 us (1%)
    pallas_call x1, Pallas kernels, block_call(): pl.pallas_call(functools.partial(block_kernel, devices), out_shape=jax.Sh...  134 us

profile of v4, /device:TPU:0, one launch (start us, length us, event | category | flops | bytes accessed | tf_op | source)
XLA Modules:
  0.0 136.2 jit_solution(1283036575364866195)
XLA Ops:
  0.0 134.5 %shard_map.82 = bf16[128,1024]{1,0:T(8,128)(2,1)} custom-call(bf16[128,2048]{1,0:T(8,128)(2,1)} %refs_0_.1, bf16[3,128,1024]{2,1,0:T(8,128)(2,1)} %bitcast.5, bf16[256,1024]{1,0:T(8,128)(2,1)} %refs_2_.1, f32[4,2048]{1,0:T(4,128)} %refs_3_.1, bf16[64,2048]{1,0:T(8,128)(2,1)} %bitcast.6, s32[4,128]{1,0:T(4,128)} %bitcast.7, ...), custom_call_target="tpu_custom_call" | custom-call | tf_op jit(solution)/shard_map/pallas_call | solution.py:674
  134.5 1.7 %copy.10 = bf16[128,1024]{1,0:T(8,128)(2,1)} copy(bf16[128,1024]{1,0:T(8,128)(2,1)} %shard_map.82) | data formatting | bytes 524288

commit v5 on v4

--- a/solution.py
+++ b/solution.py
@@ -67,6 +67,7 @@
 LANES = 128
 SLOT = 16
 COLS = 2
+PIECES = 2
 VMEM_BYTES = 66 * 1000 * 1000
 MESH = pl.DeviceIdType.MESH
 
@@ -262,98 +263,115 @@
             hid_own[h] = (gate * jax.nn.sigmoid(gate) * product(1)).astype(jnp.bfloat16)
             hid_copy(h).start()
 
-    def lower_expert(e):
+    cut = half // PIECES
+
+    def columns(c):
+        return slice(c * cut, (c + 1) * cut)
+
+    def lower_expert(e, c):
         total = None
         for b in range(2):
             h = 2 * e + b
-            weight_copies(h)[1].wait()
-            hid_copy(h).wait_recv()
-            first = dn[h, pl.ds(pl.multiple_of(part * hidden, SLOT), hidden), :]
-            second = dn[h, pl.ds(pl.multiple_of(other * hidden, SLOT), hidden), :]
+            if c == 0:
+                weight_copies(h)[1].wait()
+                hid_copy(h).wait_recv()
+            first = dn[h, pl.ds(pl.multiple_of(part * hidden, SLOT), hidden), columns(c)]
+            second = dn[h, pl.ds(pl.multiple_of(other * hidden, SLOT), hidden), columns(c)]
             piece = jnp.dot(hid_own[h], first, preferred_element_type=jnp.float32) + jnp.dot(
                 hid_other[h], second, preferred_element_type=jnp.float32
             )
             piece = piece.astype(jnp.bfloat16).astype(jnp.float32)
             total = piece if total is None else total + piece
         gain = slot_gate[e][:, :1]
-        disp[0, e] = (total * gain).astype(jnp.bfloat16)
-
-    raise_expert(0)
-
-    def step_expert(e, carry):
-        raise_expert(e)
-        lower_expert(e - 1)
-        return carry
-
-    lax.fori_loop(1, local, step_expert, 0)
-    lower_expert(local - 1)
-
-    def combine(s):
-        rows = disp[0, :, pl.ds(pl.multiple_of(s * SLOT, SLOT), SLOT), :].reshape(slots, half)
+        disp[0, e, :, columns(c)] = (total * gain).astype(jnp.bfloat16)
+
+    def each_expert(act):
+        def step(e, carry):
+            act(e)
+            return carry
+
+        lax.fori_loop(0, local, step, 0)
+
+    def combine(s, c):
+        rows = disp[0, :, pl.ds(pl.multiple_of(s * SLOT, SLOT), SLOT), columns(c)]
         return lax.dot_general(
-            pick[s], rows, (((0,), (0,)), ((), ())), preferred_element_type=jnp.float32
-        )
-
-    def x_copy(zz):
+            pick[s], rows.reshape(slots, cut), (((0,), (0,)), ((), ())),
+            preferred_element_type=jnp.float32,
+        )
+
+    def x_copy(zz, c):
         return remote(
-            tok.at[0, zz * COLS + (1 - x)], got_x.at[zz], x_s.at[zz], x_r.at[zz], x_to
-        )
-
-    def line_copy(zz, low):
+            tok.at[0, zz * COLS + (1 - x), :, columns(c)], got_x.at[zz, :, columns(c)],
+            x_s.at[zz, c], x_r.at[zz, c], x_to,
+        )
+
+    def line_copy(zz, low, c):
+        src = tok.at[1, zz, :, columns(c)]
         if low:
-            return remote(tok.at[1, zz], got_down.at[zz], down_s.at[zz], down_r.at[zz], down_to)
-        return remote(tok.at[1, zz], got_up.at[zz], up_s.at[zz], up_r.at[zz], up_to)
-
-    def give_across(zz, low):
+            return remote(
+                src, got_down.at[zz, :, columns(c)], down_s.at[zz, c], down_r.at[zz, c], down_to
+            )
+        return remote(src, got_up.at[zz, :, columns(c)], up_s.at[zz, c], up_r.at[zz, c], up_to)
+
+    def give_across(zz, c):
         s = zz * COLS + (1 - x)
-        tok[0, s] = combine(s).astype(jnp.bfloat16)
-        x_copy(zz).start()
-
-    def add_line(zz, low):
-        line_copy(zz, low).wait_recv()
-        acc[...] += (got_down if low else got_up)[zz].astype(jnp.float32)
-
-    def gather_here(zz):
-        acc[...] = combine(zz * COLS + x)
-        x_copy(zz).wait_recv()
-        acc[...] += got_x[zz].astype(jnp.float32)
-
-    def pass_on(zz, low):
-        gather_here(zz)
+        tok[0, s, :, columns(c)] = combine(s, c).astype(jnp.bfloat16)
+        x_copy(zz, c).start()
+
+    def add_line(zz, low, c):
+        line_copy(zz, low, c).wait_recv()
+        came = (got_down if low else got_up)[zz, :, columns(c)]
+        acc[:, columns(c)] += came.astype(jnp.float32)
+
+    def gather_here(zz, c):
+        acc[:, columns(c)] = combine(zz * COLS + x, c)
+        x_copy(zz, c).wait_recv()
+        acc[:, columns(c)] += got_x[zz, :, columns(c)].astype(jnp.float32)
+
+    def pass_on(zz, low, c):
+        gather_here(zz, c)
 
         @pl.when(not_top if low else not_bottom)
         def _():
-            add_line(zz, low)
-
-        tok[1, zz] = acc[...].astype(jnp.bfloat16)
-        line_copy(zz, low).start()
-
-    for d in range(lines - 1, 0, -1):
-        both(d, give_across)
-    give_across(z, False)
-    for d in range(lines - 1, 0, -1):
-        both(d, pass_on)
-    gather_here(z)
-
-    @pl.when(not_bottom)
-    def _():
-        add_line(z, False)
-
-    @pl.when(not_top)
-    def _():
-        add_line(z, True)
-
-    own = pl.ds(pl.multiple_of(part * half, LANES), half)
-    out[...] = (state[:, own] + (1.0 + modulation[3:4, own]) * acc[...]).astype(out.dtype)
-
-    for d in range(1, lines):
-
-        def drained(zz, low):
-            line_copy(zz, low).wait_send()
-            x_copy(zz).wait_send()
-
-        both(d, drained)
-    x_copy(z).wait_send()
+            add_line(zz, low, c)
+
+        tok[1, zz, :, columns(c)] = acc[:, columns(c)].astype(jnp.bfloat16)
+        line_copy(zz, low, c).start()
+
+    each_expert(raise_expert)
+    for c in range(PIECES):
+        each_expert(lambda e: lower_expert(e, c))
+        for d in range(lines - 1, 0, -1):
+            both(d, lambda zz, low: give_across(zz, c))
+        give_across(z, c)
+    for c in range(PIECES):
+        for d in range(lines - 1, 0, -1):
+            both(d, lambda zz, low: pass_on(zz, low, c))
+    for c in range(PIECES):
+        gather_here(z, c)
+
+        @pl.when(not_bottom)
+        def _():
+            add_line(z, False, c)
+
+        @pl.when(not_top)
+        def _():
+            add_line(z, True, c)
+
+        own = pl.ds(pl.multiple_of(part * half + c * cut, LANES), cut)
+        out[:, columns(c)] = (
+            state[:, own] + (1.0 + modulation[3:4, own]) * acc[:, columns(c)]
+        ).astype(out.dtype)
+
+    for c in range(PIECES):
+        for d in range(1, lines):
+
+            def drained(zz, low):
+                line_copy(zz, low, c).wait_send()
+                x_copy(zz, c).wait_send()
+
+            both(d, drained)
+        x_copy(z, c).wait_send()
     for step in range(1, devices):
         meta_copy(step).wait_send()
 
@@ -705,7 +723,7 @@
             dma((devices,)), dma((devices,)),
             dma((devices,)), dma((devices,)), dma((devices, 4)), dma((devices,)), dma((devices,)),
             dma((halves,)), dma((halves,)),
-            dma((lines,)), dma((lines,)), dma((lines,)), dma((lines,)), dma((lines,)), dma((lines,)),
+            *[dma((lines, PIECES))] * 6,
         ],
         compiler_params=pltpu.CompilerParams(
             collective_id=1, has_side_effects=True, vmem_limit_bytes=VMEM_BYTES

time: 136 us -> 137 us (level)
  no operation moved by 1% of the time
where the time goes in v5:
time: 137 us; the launch traced here: 136 us
  Pallas kernels  135 us (99%)
  local copies, waits for them, and re-layouts  1.67 us (1%)
    pallas_call x1, Pallas kernels, block_call(): pl.pallas_call(functools.partial(block_kernel, devices), out_shape=jax.Sh...  135 us

profile of v5, /device:TPU:0, one launch (start us, length us, event | category | flops | bytes accessed | tf_op | source)
XLA Modules:
  0.0 136.3 jit_solution(12827599433812646595)
XLA Ops:
  0.0 134.7 %shard_map.82 = bf16[128,1024]{1,0:T(8,128)(2,1)} custom-call(bf16[128,2048]{1,0:T(8,128)(2,1)} %refs_0_.1, bf16[3,128,1024]{2,1,0:T(8,128)(2,1)} %bitcast.5, bf16[256,1024]{1,0:T(8,128)(2,1)} %refs_2_.1, f32[4,2048]{1,0:T(4,128)} %refs_3_.1, bf16[64,2048]{1,0:T(8,128)(2,1)} %bitcast.6, s32[4,128]{1,0:T(4,128)} %bitcast.7, ...), custom_call_target="tpu_custom_call" | custom-call | tf_op jit(solution)/shard_map/pallas_call | solution.py:692
  134.7 1.7 %copy.10 = bf16[128,1024]{1,0:T(8,128)(2,1)} copy(bf16[128,1024]{1,0:T(8,128)(2,1)} %shard_map.82) | data formatting | bytes 524288
